TPU v7x, 32 devices: a whole 2x2x4 slice. The times are simulated.
32 devices in a mesh: depth: 16 (over z, x, core), freq: 2 (over y).
Axes of the slice: x: 2, y: 2, z: 4, core: 2. Of those that a mesh axis runs over, the one named last changes fastest.
Arguments:
- propagator: bfloat16 [16, 4, 2, 1024, 1024], P('depth', 'freq'), may hold values from -0.125 to 0.125
- incident: bfloat16 [16, 4, 1024, 256], P('depth', 'freq'), may hold values from -6 to 6
- coeffs: float32 [16, 1024, 64], P('depth'), may hold values from -4 to 4
Outputs:
- upgoing: bfloat16 [16, 4, 1024, 256], P('depth', 'freq')
- gradient: float32 [16, 1024, 64], P('depth', 'freq')
- reflected: bfloat16 [16, 4, 1024, 256], P('depth', 'freq')
All inputs are finite; a program needn't handle non-finite values.
Results may differ from a plain program's by a relative error of at most 0.024.
Values may be sent and summed in bfloat16 or wider, within the bound.
A program may use at most 64 MiB of HBM per device.

v0:
```python
import jax
import jax.numpy as jnp
from jax import lax
from jax.sharding import PartitionSpec as P

ITERS = 3


def passed_along(block, axis, distance):
    devices = range(lax.axis_size(axis))
    route = [(i - distance, i) for i in devices if i - distance in devices]
    return lax.ppermute(block, axis, route)


def angle_table(count, points):
    angle = jnp.arange(count, dtype=jnp.float32)[:, None] + 0.5
    place = jnp.arange(points, dtype=jnp.float32)[None, :] + 0.5
    return (jnp.sqrt(2.0 / points) * jnp.cos(jnp.pi * angle * place / points)).astype(jnp.bfloat16)


def angles_of(table, field):
    return jnp.einsum("ay,fys->fas", table, field, preferred_element_type=jnp.float32).astype(
        jnp.bfloat16
    )


def reflect(kernel, table, field):
    return jnp.einsum(
        "xa,fas->fxs", kernel, angles_of(table, field), preferred_element_type=jnp.float32
    )


def apply_level(weights, field, transpose):
    form = "fyx,fys->fxs" if transpose else "fxy,fys->fxs"
    first = jnp.einsum(form, weights[:, 0], field, preferred_element_type=jnp.float32)
    second = jnp.einsum(form, weights[:, 1], field, preferred_element_type=jnp.float32)
    half = field.shape[-1] // 2
    return first + jnp.concatenate([-second[..., half:], second[..., :half]], -1)


def local(propagator, incident, coeffs):
    weights = propagator[0]
    source = incident[0]
    count = coeffs.shape[2]
    points = incident.shape[2]
    width = incident.shape[3]
    nfreq = source.shape[0]
    table = angle_table(count, points)
    kernel = (coeffs[0] * table.T.astype(jnp.float32)).astype(jnp.bfloat16)
    down = jnp.zeros(source.shape, jnp.bfloat16)
    upgoing = jnp.zeros(source.shape, jnp.bfloat16)
    for step in range(ITERS):
        send_down = (down.astype(jnp.float32) - reflect(kernel, table, upgoing)).astype(
            jnp.bfloat16
        )
        total = (source.astype(jnp.float32) + down.astype(jnp.float32)).astype(jnp.bfloat16)
        send_up = (upgoing.astype(jnp.float32) + reflect(kernel, table, total)).astype(jnp.bfloat16)
        downs = []
        ups = []
        for index in range(nfreq):
            above = passed_along(send_down[index : index + 1], "depth", 1)
            below = passed_along(send_up[index : index + 1], "depth", -1)
            downs.append(apply_level(weights[index : index + 1], above, False).astype(jnp.bfloat16))
            ups.append(apply_level(weights[index : index + 1], below, True).astype(jnp.bfloat16))
        down = jnp.concatenate(downs, 0)
        upgoing = jnp.concatenate(ups, 0)
    total = (source.astype(jnp.float32) + down.astype(jnp.float32)).astype(jnp.bfloat16)
    final_angles = angles_of(table, total)
    scale = 1.0 / jnp.sqrt(jnp.float32(width // 2 * nfreq * lax.axis_size("freq")))
    partial_value = (
        jnp.einsum("fxs,fas->xa", upgoing, final_angles, preferred_element_type=jnp.float32) * scale
    )
    rows = points // lax.axis_size("freq")
    start = lax.axis_index("freq") * rows
    grad_rows = lax.psum_scatter(
        partial_value.astype(jnp.bfloat16), "freq", scatter_dimension=0, tiled=True
    ).astype(jnp.float32)
    mine = lax.dynamic_slice_in_dim(coeffs[0], start, rows, 0) - grad_rows
    updated = lax.all_gather(mine.astype(jnp.bfloat16), "freq", axis=0, tiled=True).astype(
        mine.dtype
    )
    new_kernel = (updated * table.T.astype(jnp.float32)).astype(jnp.bfloat16)
    reflected = jnp.einsum(
        "xa,fas->fxs", new_kernel, final_angles, preferred_element_type=jnp.float32
    ).astype(jnp.bfloat16)
    return (upgoing[None], grad_rows[None], reflected[None])


def solution(mesh):
    return jax.shard_map(
        local,
        mesh=mesh,
        in_specs=(
            P("depth", "freq", None, None, None),
            P("depth", "freq", None, None),
            P("depth", None, None),
        ),
        out_specs=(
            P("depth", "freq", None, None),
            P("depth", "freq", None),
            P("depth", "freq", None, None),
        ),
        check_vma=False,
    )
```

profile of v0, /device:TPU:0, one launch (start us, length us, event | category | flops | bytes accessed | tf_op | source)
XLA Modules:
  0.0 158.0 jit_solution(7718489618107021398)
XLA Ops:
  7.2 2.0 %fusion.115 = bf16[1024,64,1]{0,1,2:T(8,128)(2,1)S(1)} fusion(f32[1,1024,64]{1,2,0:T(8,128)} %param.5, f32[1024]{0:T(1024)S(1)} %iota_add_fusion, f32[64]{0:T(128)S(1)} %add_multiply_fusion), kind=kLoop, calls=%fused_computation.188 | loop fusion | flops 458752 | bytes 397568 | tf_op jit(solution)/shard_map/convert_element_type | solution.py:49
  11.6 3.2 %collective-permute-start.2 = (bf16[1,1024,256]{1,2,0:T(8,128)(2,1)}, bf16[1,1024,256]{1,2,0:T(8,128)(2,1)}, u32[]{:S(2)}, u32[]{:S(2)}) collective-permute-start(bf16[1,1024,256]{1,2,0:T(8,128)(2,1)} %get-tuple-element.40), channel_id=1, source_target_pairs={{0,2},{2,4},{4,6},{6,8},{8,10},{10,12},{12,14},{14,16},{16,18},{18... | collective-permute-start | bytes 1572872 | tf_op jit(solution)/shard_map/ppermute | solution.py:12
  14.8 4.5 %collective-permute-start.3 = (bf16[1,1024,256]{1,2,0:T(8,128)(2,1)S(1)}, bf16[1,1024,256]{1,2,0:T(8,128)(2,1)}, u32[]{:S(2)}, u32[]{:S(2)}) collective-permute-start(bf16[1,1024,256]{1,2,0:T(8,128)(2,1)S(1)} %get-tuple-element.41), channel_id=1, source_target_pairs={{0,2},{2,4},{4,6},{6,8},{8,10},{10,12},{12,14},{14,16},{16,18},{18... | collective-permute-start | bytes 1572872 | tf_op jit(solution)/shard_map/ppermute | solution.py:12
  24.8 3.9 %slice_bitcast_fusion.1 = (bf16[1,2,1024,1024]{3,2,1,0:T(8,128)(2,1)S(1)}, bf16[1,2,1024,1024]{3,2,1,0:T(8,128)(2,1)S(1)}) fusion(bf16[1,2,2,1024,1024]{4,3,2,1,0:T(8,128)(2,1)} %param.3), kind=kLoop, calls=%fused_computation.1 | loop fusion | bytes 16777216 | tf_op jit(solution)/shard_map/slice | solution.py:64
  28.8 2.2 %convolution_bitcast_fusion.18 = f32[1,1024,256]{1,2,0:T(8,128)S(1)} fusion(bf16[1,2,1024,1024]{3,2,1,0:T(8,128)(2,1)S(1)} %get-tuple-element.6, bf16[1,1024,256]{1,2,0:T(8,128)(2,1)} %collective-permute-done.2), kind=kOutput, calls=%fused_computation.42 | convolution fusion | flops 536870912 | bytes 3670016 | tf_op jit(solution)/shard_map/fxy,fys->fxs/dot_general | solution.py:36
  31.1 2.1 %convolution_bitcast_fusion.22 = f32[1,1024,256]{1,2,0:T(8,128)S(1)} fusion(bf16[1,2,1024,1024]{3,2,1,0:T(8,128)(2,1)S(1)} %get-tuple-element.6, bf16[1,1024,256]{1,2,0:T(8,128)(2,1)} %collective-permute-done), kind=kOutput, calls=%fused_computation.46 | convolution fusion | flops 536870912 | bytes 3670016 | tf_op jit(solution)/shard_map/fyx,fys->fxs/dot_general | solution.py:36
  33.3 1.8 %convolution_bitcast_fusion.16 = f32[1,1024,256]{1,2,0:T(8,128)S(1)} fusion(bf16[1,2,1024,1024]{3,2,1,0:T(8,128)(2,1)S(1)} %get-tuple-element.7, bf16[1,1024,256]{1,2,0:T(8,128)(2,1)} %collective-permute-done.3), kind=kOutput, calls=%fused_computation.40 | convolution fusion | flops 536870912 | bytes 3670016 | tf_op jit(solution)/shard_map/fxy,fys->fxs/dot_general | solution.py:36
  37.2 1.8 %fusion.36 = bf16[1,1024,256]{1,2,0:T(8,128)(2,1)S(1)} fusion(f32[1024,128]{0,1:T(8,128)S(1)} %get-tuple-element.39, f32[1024,128]{0,1:T(8,128)S(1)} %get-tuple-element.38, bf16[1,2,1024,1024]{3,2,1,0:T(8,128)(2,1)S(1)} %get-tuple-element.6, bf16[1,1024,256]{1,2,0:T(8,128)(2,1)} %collective-permute-done.2), kind=kOutput, calls=%fused_computation.76 | convolution fusion | flops 537657344 | bytes 4194304 | tf_op jit(solution)/shard_map/fxy,fys->fxs/dot_general | solution.py:35
  39.0 2.8 %fusion.34 = bf16[1,1024,256]{1,2,0:T(8,128)(2,1)} fusion(f32[1024,128]{0,1:T(8,128)S(1)} %get-tuple-element.33, f32[1024,128]{0,1:T(8,128)S(1)} %get-tuple-element.32, bf16[1,2,1024,1024]{3,2,1,0:T(8,128)(2,1)S(1)} %get-tuple-element.6, bf16[1,1024,256]{1,2,0:T(8,128)(2,1)} %collective-permute-done), kind=kOutput, calls=%fused_computation.74 | convolution fusion | flops 537657344 | bytes 4194304 | tf_op jit(solution)/shard_map/fyx,fys->fxs/dot_general | solution.py:35
  41.8 2.6 %fusion.37 = bf16[1,1024,256]{1,2,0:T(8,128)(2,1)} fusion(f32[1024,128]{0,1:T(8,128)S(1)} %get-tuple-element.43, f32[1024,128]{0,1:T(8,128)S(1)} %get-tuple-element.42, bf16[1,2,1024,1024]{3,2,1,0:T(8,128)(2,1)S(1)} %get-tuple-element.7, bf16[1,1024,256]{1,2,0:T(8,128)(2,1)} %collective-permute-done.3), kind=kOutput, calls=%fused_computation.77 | convolution fusion | flops 537657344 | bytes 4194304 | tf_op jit(solution)/shard_map/fxy,fys->fxs/dot_general | solution.py:35
  44.4 2.7 %fusion.35 = bf16[1,1024,256]{1,2,0:T(8,128)(2,1)} fusion(f32[1024,128]{0,1:T(8,128)S(1)} %get-tuple-element.37, f32[1024,128]{0,1:T(8,128)S(1)} %get-tuple-element.36, bf16[1,2,1024,1024]{3,2,1,0:T(8,128)(2,1)S(1)} %get-tuple-element.7, bf16[1,1024,256]{1,2,0:T(8,128)(2,1)} %collective-permute-done.1), kind=kOutput, calls=%fused_computation.75 | convolution fusion | flops 537657344 | bytes 4194304 | tf_op jit(solution)/shard_map/fyx,fys->fxs/dot_general | solution.py:35
  47.1 2.9 %fusion.6 = bf16[2,1024,256]{1,2,0:T(8,128)(2,1)S(1)} fusion(bf16[1024,64,1]{0,1,2:T(8,128)(2,1)S(1)} %fusion.115, bf16[1,2,1024,256]{2,3,1,0:T(8,128)(2,1)S(1)} %copy.6, bf16[1,1024,256]{1,2,0:T(8,128)(2,1)} %fusion.37, bf16[1,1024,256]{1,2,0:T(8,128)(2,1)S(1)} %fusion.36, bf16[1,1024,256]{1,2,0:T(8,128)(2,1)} %fusion.35, ...), kind=kOutput, calls=%fused_computation.19 | convolution fusion | flops 140279808 | bytes 4329728 | tf_op jit(solution)/shard_map/xa,fas->fxs/dot_general | solution.py:28
  51.6 3.1 %fusion = bf16[2,1024,256]{1,2,0:T(8,128)(2,1)S(1)} fusion(bf16[1024,64,1]{0,1,2:T(8,128)(2,1)S(1)} %fusion.115, bf16[1,1024,256]{1,2,0:T(8,128)(2,1)} %fusion.37, bf16[1,1024,256]{1,2,0:T(8,128)(2,1)} %copy-done.10, bf16[1,1024,256]{1,2,0:T(8,128)(2,1)} %fusion.35, bf16[1,1024,256]{1,2,0:T(8,128)(2,1)} %fusion.34, f32[1024]{0:T(1024)S(1)} %iota_add_fusion, ...), kind=kOutput, calls=%fused_computation.7 | convolution fusion | flops 138182656 | bytes 3281152 | tf_op jit(solution)/shard_map/xa,fas->fxs/dot_general | solution.py:28
  54.8 9.0 %collective-permute-start.6 = (bf16[1,1024,256]{1,2,0:T(8,128)(2,1)S(1)}, bf16[1,1024,256]{1,2,0:T(8,128)(2,1)S(1)}, u32[]{:S(2)}, u32[]{:S(2)}) collective-permute-start(bf16[1,1024,256]{1,2,0:T(8,128)(2,1)S(1)} %get-tuple-element.28), channel_id=1, source_target_pairs={{0,2},{2,4},{4,6},{6,8},{8,10},{10,12},{12,14},{14,16},{16,18},{18... | collective-permute-start | bytes 1572872 | tf_op jit(solution)/shard_map/ppermute | solution.py:12
  63.8 4.5 %collective-permute-start.7 = (bf16[1,1024,256]{1,2,0:T(8,128)(2,1)S(1)}, bf16[1,1024,256]{1,2,0:T(8,128)(2,1)S(1)}, u32[]{:S(2)}, u32[]{:S(2)}) collective-permute-start(bf16[1,1024,256]{1,2,0:T(8,128)(2,1)S(1)} %get-tuple-element.29), channel_id=1, source_target_pairs={{0,2},{2,4},{4,6},{6,8},{8,10},{10,12},{12,14},{14,16},{16,18},{18... | collective-permute-start | bytes 1572872 | tf_op jit(solution)/shard_map/ppermute | solution.py:12
  69.9 2.5 %convolution_bitcast_fusion.12 = f32[1,1024,256]{1,2,0:T(8,128)S(1)} fusion(bf16[1,2,1024,1024]{3,2,1,0:T(8,128)(2,1)} %copy-done.4, bf16[1,1024,256]{1,2,0:T(8,128)(2,1)} %collective-permute-done.5), kind=kOutput, calls=%fused_computation.36 | convolution fusion | flops 536870912 | bytes 3670016 | tf_op jit(solution)/shard_map/fyx,fys->fxs/dot_general | solution.py:36
  82.0 3.0 %fusion.5 = bf16[2,1024,256]{1,2,0:T(8,128)(2,1)S(1)} fusion(bf16[1024,64,1]{0,1,2:T(8,128)(2,1)S(1)} %fusion.115, bf16[1,2,1024,256]{2,3,1,0:T(8,128)(2,1)S(1)} %copy.6, bf16[1,1024,256]{1,2,0:T(8,128)(2,1)} %fusion.41, bf16[1,1024,256]{1,2,0:T(8,128)(2,1)} %fusion.40, bf16[1,1024,256]{1,2,0:T(8,128)(2,1)S(1)} %fusion.39, ...), kind=kOutput, calls=%fused_computation.17 | convolution fusion | flops 140279808 | bytes 4329728 | tf_op jit(solution)/shard_map/xa,fas->fxs/dot_general | solution.py:28
  86.4 3.1 %fusion.1 = bf16[2,1024,256]{1,2,0:T(8,128)(2,1)S(1)} fusion(bf16[1024,64,1]{0,1,2:T(8,128)(2,1)S(1)} %fusion.115, bf16[1,1024,256]{1,2,0:T(8,128)(2,1)} %fusion.41, bf16[1,1024,256]{1,2,0:T(8,128)(2,1)} %fusion.40, bf16[1,1024,256]{1,2,0:T(8,128)(2,1)} %copy-done.9, bf16[1,1024,256]{1,2,0:T(8,128)(2,1)} %copy-done.11, f32[1024]{0:T(1024)S(1)} %iota_add_fusion, ...), kind=kOutput, calls=%fused_computation.8 | convolution fusion | flops 138182656 | bytes 3281152 | tf_op jit(solution)/shard_map/xa,fas->fxs/dot_general | solution.py:28
  89.5 11.7 %collective-permute-start.10 = (bf16[1,1024,256]{1,2,0:T(8,128)(2,1)S(1)}, bf16[1,1024,256]{1,2,0:T(8,128)(2,1)S(1)}, u32[]{:S(2)}, u32[]{:S(2)}) collective-permute-start(bf16[1,1024,256]{1,2,0:T(8,128)(2,1)S(1)} %get-tuple-element.10), channel_id=1, source_target_pairs={{0,2},{2,4},{4,6},{6,8},{8,10},{10,12},{12,14},{14,16},{16,18},{18... | collective-permute-start | bytes 1572872 | tf_op jit(solution)/shard_map/ppermute | solution.py:12
  101.2 4.4 %collective-permute-start.11 = (bf16[1,1024,256]{1,2,0:T(8,128)(2,1)S(1)}, bf16[1,1024,256]{1,2,0:T(8,128)(2,1)S(1)}, u32[]{:S(2)}, u32[]{:S(2)}) collective-permute-start(bf16[1,1024,256]{1,2,0:T(8,128)(2,1)S(1)} %get-tuple-element.11), channel_id=1, source_target_pairs={{0,2},{2,4},{4,6},{6,8},{8,10},{10,12},{12,14},{14,16},{16,18},{18... | collective-permute-start | bytes 1572872 | tf_op jit(solution)/shard_map/ppermute | solution.py:12
  105.7 1.8 %collective-permute-start.8 = (bf16[1,1024,256]{1,2,0:T(8,128)(2,1)S(1)}, bf16[1,1024,256]{1,2,0:T(8,128)(2,1)S(1)}, u32[]{:S(2)}, u32[]{:S(2)}) collective-permute-start(bf16[1,1024,256]{1,2,0:T(8,128)(2,1)S(1)} %get-tuple-element.16), channel_id=1, source_target_pairs={{2,0},{4,2},{6,4},{8,6},{10,8},{12,10},{14,12},{16,14},{18,16},{20... | collective-permute-start | bytes 1572872 | tf_op jit(solution)/shard_map/ppermute | solution.py:12
  107.5 2.5 %convolution_bitcast_fusion.4 = f32[1,1024,256]{1,2,0:T(8,128)S(1)} fusion(bf16[1,2,1024,1024]{3,2,1,0:T(8,128)(2,1)} %copy-done.4, bf16[1,1024,256]{1,2,0:T(8,128)(2,1)} %collective-permute-done.9), kind=kOutput, calls=%fused_computation.28 | convolution fusion | flops 536870912 | bytes 3670016 | tf_op jit(solution)/shard_map/fyx,fys->fxs/dot_general | solution.py:36
  121.6 20.4 %reduce-scatter.2.cloned.1.call-done = bf16[512,64]{0,1:T(8,128)(2,1)} async-done(((bf16[1024,64]{0,1:T(8,128)(2,1)}), bf16[512,64]{0,1:T(8,128)(2,1)}) %reduce-scatter.2.cloned.1.call-update) | async-done | bytes 65552 | tf_op jit(solution)/shard_map/reduce_scatter | solution.py:75
  142.9 4.9 %all_gather.3 = bf16[1024,64]{0,1:T(8,128)(2,1)S(1)} all-gather(bf16[512,64]{0,1:T(8,128)(2,1)S(1)} %fusion.111), channel_id=1, replica_groups=mesh['depth'=16,'freq'=2] {'freq'}, dimensions={0}, use_global_device_ids=true | all-gather | bytes 196608 | tf_op jit(solution)/shard_map/all_gather | solution.py:79
  (91 shorter events, 39.8 us)
Async XLA Ops:
  7.2 12.2 %copy-start = (bf16[1,2,1024,256]{3,2,1,0:T(8,128)(2,1)S(1)}, bf16[1,2,1024,256]{3,2,1,0:T(8,128)(2,1)}, u32[]{:S(2)}) copy-start(bf16[1,2,1024,256]{3,2,1,0:T(8,128)(2,1)} %param.4) | copy-start | bytes 3145732
  7.2 134.8 %reduce-scatter.2.cloned.1.call-start = ((), (), s32[]{:S(2)}) async-start(), calls=%async_computation.1 | async-start | bytes 196608 | tf_op jit(solution)/shard_map/reduce_scatter | solution.py:75
  11.6 17.2 %collective-permute-start.2 = (bf16[1,1024,256]{1,2,0:T(8,128)(2,1)}, bf16[1,1024,256]{1,2,0:T(8,128)(2,1)}, u32[]{:S(2)}, u32[]{:S(2)}) collective-permute-start(bf16[1,1024,256]{1,2,0:T(8,128)(2,1)} %get-tuple-element.40), channel_id=1, source_target_pairs={{0,2},{2,4},{4,6},{6,8},{8,10},{10,12},{12,14},{14,16},{16,18},{18... | collective-permute-start | bytes 1572872 | tf_op jit(solution)/shard_map/ppermute | solution.py:12
  14.8 18.5 %collective-permute-start.3 = (bf16[1,1024,256]{1,2,0:T(8,128)(2,1)S(1)}, bf16[1,1024,256]{1,2,0:T(8,128)(2,1)}, u32[]{:S(2)}, u32[]{:S(2)}) collective-permute-start(bf16[1,1024,256]{1,2,0:T(8,128)(2,1)S(1)} %get-tuple-element.41), channel_id=1, source_target_pairs={{0,2},{2,4},{4,6},{6,8},{8,10},{10,12},{12,14},{14,16},{16,18},{18... | collective-permute-start | bytes 1572872 | tf_op jit(solution)/shard_map/ppermute | solution.py:12
  21.7 9.4 %collective-permute-start = (bf16[1,1024,256]{1,2,0:T(8,128)(2,1)}, bf16[1,1024,256]{1,2,0:T(8,128)(2,1)}, u32[]{:S(2)}, u32[]{:S(2)}) collective-permute-start(bf16[1,1024,256]{1,2,0:T(8,128)(2,1)} %get-tuple-element.34), channel_id=1, source_target_pairs={{2,0},{4,2},{6,4},{8,6},{10,8},{12,10},{14,12},{16,14},{18,16},{20... | collective-permute-start | bytes 1572872 | tf_op jit(solution)/shard_map/ppermute | solution.py:12
  23.0 12.3 %collective-permute-start.1 = (bf16[1,1024,256]{1,2,0:T(8,128)(2,1)S(1)}, bf16[1,1024,256]{1,2,0:T(8,128)(2,1)}, u32[]{:S(2)}, u32[]{:S(2)}) collective-permute-start(bf16[1,1024,256]{1,2,0:T(8,128)(2,1)S(1)} %get-tuple-element.35), channel_id=1, source_target_pairs={{2,0},{4,2},{6,4},{8,6},{10,8},{12,10},{14,12},{16,14},{18,16},{20... | collective-permute-start | bytes 1572872 | tf_op jit(solution)/shard_map/ppermute | solution.py:12
  28.8 10.2 %copy-start.1 = (bf16[1,2,1024,1024]{3,2,1,0:T(8,128)(2,1)}, bf16[1,2,1024,1024]{3,2,1,0:T(8,128)(2,1)S(1)}, u32[]{:S(2)}) copy-start(bf16[1,2,1024,1024]{3,2,1,0:T(8,128)(2,1)S(1)} %get-tuple-element.6) | copy-start | bytes 12582916
  28.8 15.6 %copy-start.4 = (bf16[1,2,1024,1024]{3,2,1,0:T(8,128)(2,1)}, bf16[1,2,1024,1024]{3,2,1,0:T(8,128)(2,1)S(1)}, u32[]{:S(2)}) copy-start(bf16[1,2,1024,1024]{3,2,1,0:T(8,128)(2,1)S(1)} %get-tuple-element.7) | copy-start | bytes 12582916
  39.0 8.1 %copy-start.10 = (bf16[1,1024,256]{1,2,0:T(8,128)(2,1)}, bf16[1,1024,256]{1,2,0:T(8,128)(2,1)S(1)}, u32[]{:S(2)}) copy-start(bf16[1,1024,256]{1,2,0:T(8,128)(2,1)S(1)} %fusion.36) | copy-start | bytes 1572868
  44.4 2.7 %copy-start.12 = (bf16[1,1024,256]{1,2,0:T(8,128)(2,1)S(1)}, bf16[1,1024,256]{1,2,0:T(8,128)(2,1)}, u32[]{:S(2)}) copy-start(bf16[1,1024,256]{1,2,0:T(8,128)(2,1)} %fusion.34) | copy-start | bytes 1572868
  50.1 19.8 %collective-permute-start.5 = (bf16[1,1024,256]{1,2,0:T(8,128)(2,1)S(1)}, bf16[1,1024,256]{1,2,0:T(8,128)(2,1)}, u32[]{:S(2)}, u32[]{:S(2)}) collective-permute-start(bf16[1,1024,256]{1,2,0:T(8,128)(2,1)S(1)} %get-tuple-element.23), channel_id=1, source_target_pairs={{2,0},{4,2},{6,4},{8,6},{10,8},{12,10},{14,12},{16,14},{18,16},{20... | collective-permute-start | bytes 1572872 | tf_op jit(solution)/shard_map/ppermute | solution.py:12
  54.8 20.8 %collective-permute-start.6 = (bf16[1,1024,256]{1,2,0:T(8,128)(2,1)S(1)}, bf16[1,1024,256]{1,2,0:T(8,128)(2,1)S(1)}, u32[]{:S(2)}, u32[]{:S(2)}) collective-permute-start(bf16[1,1024,256]{1,2,0:T(8,128)(2,1)S(1)} %get-tuple-element.28), channel_id=1, source_target_pairs={{0,2},{2,4},{4,6},{6,8},{8,10},{10,12},{12,14},{14,16},{16,18},{18... | collective-permute-start | bytes 1572872 | tf_op jit(solution)/shard_map/ppermute | solution.py:12
  63.8 9.4 %collective-permute-start.7 = (bf16[1,1024,256]{1,2,0:T(8,128)(2,1)S(1)}, bf16[1,1024,256]{1,2,0:T(8,128)(2,1)S(1)}, u32[]{:S(2)}, u32[]{:S(2)}) collective-permute-start(bf16[1,1024,256]{1,2,0:T(8,128)(2,1)S(1)} %get-tuple-element.29), channel_id=1, source_target_pairs={{0,2},{2,4},{4,6},{6,8},{8,10},{10,12},{12,14},{14,16},{16,18},{18... | collective-permute-start | bytes 1572872 | tf_op jit(solution)/shard_map/ppermute | solution.py:12
  68.3 4.2 %copy-start.2 = (bf16[1,2,1024,1024]{3,2,1,0:T(8,128)(2,1)S(1)}, bf16[1,2,1024,1024]{3,2,1,0:T(8,128)(2,1)}, u32[]{:S(2)}) copy-start(bf16[1,2,1024,1024]{3,2,1,0:T(8,128)(2,1)} %copy-done.1) | copy-start | bytes 12582916
  68.3 4.2 %collective-permute-start.4 = (bf16[1,1024,256]{1,2,0:T(8,128)(2,1)S(1)}, bf16[1,1024,256]{1,2,0:T(8,128)(2,1)S(1)}, u32[]{:S(2)}, u32[]{:S(2)}) collective-permute-start(bf16[1,1024,256]{1,2,0:T(8,128)(2,1)S(1)} %get-tuple-element.22), channel_id=1, source_target_pairs={{2,0},{4,2},{6,4},{8,6},{10,8},{12,10},{14,12},{16,14},{18,16},{20... | collective-permute-start | bytes 1572872 | tf_op jit(solution)/shard_map/ppermute | solution.py:12
  78.2 3.8 %copy-start.9 = (bf16[1,1024,256]{1,2,0:T(8,128)(2,1)}, bf16[1,1024,256]{1,2,0:T(8,128)(2,1)S(1)}, u32[]{:S(2)}) copy-start(bf16[1,1024,256]{1,2,0:T(8,128)(2,1)S(1)} %fusion.39) | copy-start | bytes 1572868
  78.9 3.1 %copy-start.11 = (bf16[1,1024,256]{1,2,0:T(8,128)(2,1)}, bf16[1,1024,256]{1,2,0:T(8,128)(2,1)S(1)}, u32[]{:S(2)}) copy-start(bf16[1,1024,256]{1,2,0:T(8,128)(2,1)S(1)} %fusion.38) | copy-start | bytes 1572868
  85.1 22.4 %collective-permute-start.9 = (bf16[1,1024,256]{1,2,0:T(8,128)(2,1)S(1)}, bf16[1,1024,256]{1,2,0:T(8,128)(2,1)}, u32[]{:S(2)}, u32[]{:S(2)}) collective-permute-start(bf16[1,1024,256]{1,2,0:T(8,128)(2,1)S(1)} %get-tuple-element.17), channel_id=1, source_target_pairs={{2,0},{4,2},{6,4},{8,6},{10,8},{12,10},{14,12},{16,14},{18,16},{20... | collective-permute-start | bytes 1572872 | tf_op jit(solution)/shard_map/ppermute | solution.py:12
  89.5 23.5 %collective-permute-start.10 = (bf16[1,1024,256]{1,2,0:T(8,128)(2,1)S(1)}, bf16[1,1024,256]{1,2,0:T(8,128)(2,1)S(1)}, u32[]{:S(2)}, u32[]{:S(2)}) collective-permute-start(bf16[1,1024,256]{1,2,0:T(8,128)(2,1)S(1)} %get-tuple-element.10), channel_id=1, source_target_pairs={{0,2},{2,4},{4,6},{6,8},{8,10},{10,12},{12,14},{14,16},{16,18},{18... | collective-permute-start | bytes 1572872 | tf_op jit(solution)/shard_map/ppermute | solution.py:12
  101.2 9.5 %collective-permute-start.11 = (bf16[1,1024,256]{1,2,0:T(8,128)(2,1)S(1)}, bf16[1,1024,256]{1,2,0:T(8,128)(2,1)S(1)}, u32[]{:S(2)}, u32[]{:S(2)}) collective-permute-start(bf16[1,1024,256]{1,2,0:T(8,128)(2,1)S(1)} %get-tuple-element.11), channel_id=1, source_target_pairs={{0,2},{2,4},{4,6},{6,8},{8,10},{10,12},{12,14},{14,16},{16,18},{18... | collective-permute-start | bytes 1572872 | tf_op jit(solution)/shard_map/ppermute | solution.py:12
  105.6 4.4 %copy-start.3 = (bf16[1,2,1024,1024]{3,2,1,0:T(8,128)(2,1)S(1)}, bf16[1,2,1024,1024]{3,2,1,0:T(8,128)(2,1)}, u32[]{:S(2)}) copy-start(bf16[1,2,1024,1024]{3,2,1,0:T(8,128)(2,1)} %copy-done.1) | copy-start | bytes 12582916
  105.7 4.4 %collective-permute-start.8 = (bf16[1,1024,256]{1,2,0:T(8,128)(2,1)S(1)}, bf16[1,1024,256]{1,2,0:T(8,128)(2,1)S(1)}, u32[]{:S(2)}, u32[]{:S(2)}) collective-permute-start(bf16[1,1024,256]{1,2,0:T(8,128)(2,1)S(1)} %get-tuple-element.16), channel_id=1, source_target_pairs={{2,0},{4,2},{6,4},{8,6},{10,8},{12,10},{14,12},{16,14},{18,16},{20... | collective-permute-start | bytes 1572872 | tf_op jit(solution)/shard_map/ppermute | solution.py:12
  120.1 21.9 %copy-start.7 = (f32[1,1024,64]{1,2,0:T(8,128)S(1)}, f32[1,1024,64]{1,2,0:T(8,128)}, u32[]{:S(2)}) copy-start(f32[1,1024,64]{1,2,0:T(8,128)} %param.5) | copy-start | bytes 786436
  142.0 8.5 %copy-start.8 = (bf16[512,64]{0,1:T(8,128)(2,1)S(1)}, bf16[512,64]{0,1:T(8,128)(2,1)}, u32[]{:S(2)}) copy-start(bf16[512,64]{0,1:T(8,128)(2,1)} %reduce-scatter.2.cloned.1.call-done) | copy-start | bytes 196612
  (2 other events, 4.4 us)
Sparse Core Ops, SparseCore 0:
  120.2 21.6 reduce-scatter.1
where the time goes:
time: 159 us; the launch traced here: 158 us
  matrix products  55.3 us (35%)
  starting transfers between devices  46.1 us (29%)
  waiting for transfers between devices  20.5 us (13%)
  between operations  14.7 us (9%)
  local copies, waits for them, and re-layouts  11.8 us (7%)
  blocking collectives  4.93 us (3%)
  other arithmetic  4.72 us (3%)
    ppermute x12, starting transfers between devices, passed_along(): return lax.ppermute(block, axis, route)  46 us
    reduce_scatter x1, waiting for transfers between devices, local(): lax.psum_scatter(partial_value.astype(jnp.bfloat16), 'freq', scatter_dime...  20.4 us
    dot_general x12, matrix products, apply_level(): jnp.einsum(form, weights[:, 0], field, preferred_element_type=jnp.float32)  19.4 us
    dot_general x12, matrix products, apply_level(): jnp.einsum(form, weights[:, 1], field, preferred_element_type=jnp.float32)  17.3 us
    dot_general x6, matrix products, reflect(): jnp.einsum('xa,fas->fxs', kernel, angles_of(table, field), preferred_elem...  15.1 us
    unnamed x29, local copies, waits for them, and re-layouts  5.9 us
    all_gather x1, blocking collectives, local(): lax.all_gather(mine.astype(jnp.bfloat16), 'freq', axis=0, tiled=True)  4.93 us
    slice x1, local copies, waits for them, and re-layouts, local(): weights[index:index + 1]  3.94 us
  transfers between devices with their start and end apart: 13, of which 1 were waited for; matrix products, arithmetic and copies ran while one was open for 19% of the time, Pallas kernels for 0%

commit v1 on v0

v1 whole, which is shorter than its diff:
```python
import jax
import jax.numpy as jnp
from jax import lax
from jax.sharding import PartitionSpec as P

BF = jnp.bfloat16
F32 = jnp.float32


def passed_along(block, axis, distance):
    devices = range(lax.axis_size(axis))
    route = [(i - distance, i) for i in devices if i - distance in devices]
    return lax.ppermute(block, axis, route)


def angle_table(count, points):
    angle = jnp.arange(count, dtype=F32)[:, None] + 0.5
    place = jnp.arange(points, dtype=F32)[None, :] + 0.5
    return (jnp.sqrt(2.0 / points) * jnp.cos(jnp.pi * angle * place / points)).astype(BF)


def dot(a, b):
    return jnp.dot(a, b, preferred_element_type=F32)


def dot_nt(a, b):
    return lax.dot_general(a, b, (((1,), (1,)), ((), ())), preferred_element_type=F32)


def dot_tn(a, b):
    return lax.dot_general(a, b, (((0,), (0,)), ((), ())), preferred_element_type=F32)


def turned(field):
    half = field.shape[-1] // 2
    return jnp.concatenate([-field[:, half:], field[:, :half]], 1)


def paired(field):
    return jnp.concatenate([field, turned(field)], 0)


def complex_rows(rows, real, imag):
    half = rows.shape[0] // 2
    first = dot(rows, real)
    second = dot(rows, imag)
    return (
        (first[:half] - second[half:]).astype(BF),
        (first[half:] + second[:half]).astype(BF),
    )


def small(table, real, imag):
    return jnp.concatenate([dot_nt(table, real), dot_nt(table, imag)], 1).astype(BF)


def local(propagator, incident, coeffs):
    weights = propagator[0]
    source = incident[0]
    count = coeffs.shape[2]
    points = incident.shape[2]
    width = incident.shape[3]
    nfreq = source.shape[0]
    table = angle_table(count, points)
    kernel = (coeffs[0].T * table.astype(F32)).astype(BF)
    kernel_up = passed_along(kernel, "depth", -1)
    kernel_down = passed_along(kernel, "depth", 1)
    outs = []
    finals = []
    partial_value = 0.0
    for f in range(nfreq):
        real, imag = weights[f, 0], weights[f, 1]
        a0 = dot(table, source[f]).astype(BF)
        a1 = passed_along(a0, "depth", -1)
        a2 = passed_along(a1, "depth", -1)
        a3 = passed_along(a2, "depth", -1)
        lhs = jnp.concatenate([kernel_up, table], 0)
        one = jnp.concatenate([dot(lhs, real), dot(lhs, imag)], 0).astype(BF)
        g1r, g1i = one[:count], one[2 * count : 3 * count]
        one_up = passed_along(one, "depth", -1)
        s1r_up, s1i_up = one_up[count : 2 * count], one_up[3 * count :]
        two_r, two_i = complex_rows(one_up, real, imag)
        g2r, s2r = two_r[:count], two_r[count:]
        g2i, s2i = two_i[:count], two_i[count:]
        g2_up = passed_along(jnp.concatenate([g2r, g2i], 0), "depth", -1)
        g3r, g3i = complex_rows(g2_up, real, imag)
        tg1 = small(table, g1r, g1i)
        tg2 = small(table, g2r, g2i)
        b0 = dot(tg1, paired(a1)).astype(BF)
        b_down = passed_along(b0, "depth", 1)
        c0 = (dot(tg2, paired(a2)) + dot(tg1, paired(a1))).astype(BF)
        th1 = jnp.concatenate([dot_nt(s1r_up, kernel), dot_nt(s1i_up, kernel)], 1).astype(BF)
        th2 = jnp.concatenate([dot_nt(s2r, kernel_down), dot_nt(s2i, kernel_down)], 1).astype(BF)
        d1 = (a1.astype(F32) - dot(th1, paired(b0))).astype(BF)
        e1 = (dot(th2, paired(b_down)) + dot(th1, paired(c0))).astype(BF)
        e0 = passed_along(e1, "depth", 1)
        final = (a0.astype(F32) - e0.astype(F32)).astype(BF)
        up = dot_tn(
            jnp.concatenate([g3r, g3i, g2r, g2i, g1r, g1i], 0),
            jnp.concatenate([paired(a3), paired(a2), paired(d1)], 0),
        ).astype(BF)
        outs.append(up)
        finals.append(final)
        partial_value = partial_value + dot_nt(up, final)
    upgoing = jnp.stack(outs)
    scale = 1.0 / jnp.sqrt(F32(width // 2 * nfreq * lax.axis_size("freq")))
    partial_value = partial_value * scale
    rows = points // lax.axis_size("freq")
    start = lax.axis_index("freq") * rows
    grad_rows = lax.psum_scatter(
        partial_value.astype(BF), "freq", scatter_dimension=0, tiled=True
    ).astype(F32)
    mine = lax.dynamic_slice_in_dim(coeffs[0], start, rows, 0) - grad_rows
    updated = lax.all_gather(mine.astype(BF), "freq", axis=0, tiled=True).astype(mine.dtype)
    new_kernel = (updated * table.T.astype(F32)).astype(BF)
    reflected = jnp.stack([dot(new_kernel, final).astype(BF) for final in finals])
    return (upgoing[None], grad_rows[None], reflected[None])


def solution(mesh):
    return jax.shard_map(
        local,
        mesh=mesh,
        in_specs=(
            P("depth", "freq", None, None, None),
            P("depth", "freq", None, None),
            P("depth", None, None),
        ),
        out_specs=(
            P("depth", "freq", None, None),
            P("depth", "freq", None),
            P("depth", "freq", None, None),
        ),
        check_vma=False,
    )
```

time: 159 us -> 130 us (0.82)
  matrix products: 55.3 us -> 30.4 us
  waiting for transfers between devices: 20.5 us -> 33.1 us
  local copies, waits for them, and re-layouts: 11.8 us -> 0.16 us
  starting transfers between devices: 46.1 us -> 38.5 us
  other arithmetic: 4.72 us -> 7.34 us
    dot_general x33 -> x46, matrix products: 55.3 us -> 30.4 us  [the longest x26 18.4 us: dot(): return jnp.dot(a, b, preferred_element_type=F32)]
    ppermute x12 -> x16, waiting for transfers between devices: 0.03 us -> 17.7 us  [passed_along(): return lax.ppermute(block, axis, route)]
    ppermute x12 -> x16, starting transfers between devices: 46 us -> 38.5 us  [passed_along(): return lax.ppermute(block, axis, route)]
    slice x7 -> x4, local copies, waits for them, and re-layouts: 5.94 us -> 0.04 us  [the longest x2 0.02 us: local(): g2i, s2i = (two_i[:count], two_i[count:])]
    unnamed x29 -> x14, local copies, waits for them, and re-layouts: 5.9 us -> 0.09 us
    reduce_scatter x1, waiting for transfers between devices: 20.4 us -> 15.4 us  [local(): lax.psum_scatter(partial_value.astype(BF), 'freq', scatter_dimension=0, t...]
    broadcast_in_dim x2 -> x3, other arithmetic: 0.76 us -> 3.63 us  [local(): return (upgoing[None], grad_rows[None], reflected[None])]
    convert_element_type x2 -> x4, other arithmetic: 2.89 us -> 3.32 us  [the longest x1 2.05 us: local(): kernel = (coeffs[0].T * table.astype(F32)).astype(BF)]
  transfers between devices with their start and end apart: 13 -> 17, of which waited for: 1 -> 9; matrix products, arithmetic and copies ran while one was open for 19% -> 22% of each run, Pallas kernels for 0% -> 0%
where the time goes in v1:
time: 130 us; the launch traced here: 129 us
  starting transfers between devices  38.5 us (30%)
  waiting for transfers between devices  33.1 us (25%)
  matrix products  30.4 us (23%)
  between operations  14.8 us (11%)
  other arithmetic  7.34 us (6%)
  blocking collectives  5.15 us (4%)
    ppermute x16, starting transfers between devices, passed_along(): return lax.ppermute(block, axis, route)  38.5 us
    dot_general x26, matrix products, dot(): return jnp.dot(a, b, preferred_element_type=F32)  18.4 us
    ppermute x16, waiting for transfers between devices, passed_along(): return lax.ppermute(block, axis, route)  17.7 us
    reduce_scatter x1, waiting for transfers between devices, local(): lax.psum_scatter(partial_value.astype(BF), 'freq', scatter_dimension=0, t...  15.4 us
    dot_general x18, matrix products, dot_nt(): lax.dot_general(a, b, (((1,), (1,)), ((), ())), preferred_element_type=F32)  11.1 us
    all_gather x1, blocking collectives, local(): lax.all_gather(mine.astype(BF), 'freq', axis=0, tiled=True)  5.15 us
    broadcast_in_dim x3, other arithmetic, local(): return (upgoing[None], grad_rows[None], reflected[None])  3.63 us
  transfers between devices with their start and end apart: 17, of which 9 were waited for; matrix products, arithmetic and copies ran while one was open for 22% of the time, Pallas kernels for 0%

profile of v1, /device:TPU:0, one launch (start us, length us, event | category | flops | bytes accessed | tf_op | source)
XLA Modules:
  0.0 129.5 jit_solution(6043243686327361307)
XLA Ops:
  7.2 2.1 %fusion.36 = (bf16[64,1024]{1,0:T(8,128)(2,1)S(1)}, bf16[64,1024]{1,0:T(8,128)(2,1)S(1)}) fusion(f32[1,1024,64]{1,2,0:T(8,128)} %param.5, f32[1024]{0:T(1024)S(1)} %iota_add_fusion, f32[64]{0:T(128)S(1)} %add_multiply_fusion), kind=kLoop, calls=%fused_computation.83 | loop fusion | flops 458752 | bytes 528640 | tf_op jit(solution)/shard_map/convert_element_type | solution.py:65
  9.3 1.4 %collective-permute-start = (bf16[64,1024]{1,0:T(8,128)(2,1)S(1)}, bf16[64,1024]{1,0:T(8,128)(2,1)S(1)}, u32[]{:S(2)}, u32[]{:S(2)}) collective-permute-start(bf16[64,1024]{1,0:T(8,128)(2,1)S(1)} %get-tuple-element.35), channel_id=1, source_target_pairs={{2,0},{4,2},{6,4},{8,6},{10,8},{12,10},{14,12},{16,14},{18,16},{20... | collective-permute-start | bytes 393224 | tf_op jit(solution)/shard_map/ppermute | solution.py:13
  10.7 3.0 %collective-permute-start.11 = (bf16[64,1024]{1,0:T(8,128)(2,1)S(1)}, bf16[64,1024]{1,0:T(8,128)(2,1)S(1)}, u32[]{:S(2)}, u32[]{:S(2)}) collective-permute-start(bf16[64,1024]{1,0:T(8,128)(2,1)S(1)} %get-tuple-element.35), channel_id=1, source_target_pairs={{0,2},{2,4},{4,6},{6,8},{8,10},{10,12},{12,14},{14,16},{16,18},{18... | collective-permute-start | bytes 393224 | tf_op jit(solution)/shard_map/ppermute | solution.py:13
  13.8 2.1 %convolution_convert_fusion.5 = bf16[64,256]{1,0:T(8,128)(2,1)S(1)} fusion(bf16[1,2,1024,256]{3,2,1,0:T(8,128)(2,1)} %param.4, f32[1024]{0:T(1024)S(1)} %iota_add_fusion, f32[64]{0:T(128)S(1)} %add_multiply_fusion), kind=kOutput, calls=%fused_computation.38 | convolution fusion | flops 33832960 | bytes 561408 | tf_op jit(solution)/shard_map/dot_general | solution.py:23
  15.9 1.3 %collective-permute-start.3 = (bf16[64,256]{1,0:T(8,128)(2,1)S(1)}, bf16[64,256]{1,0:T(8,128)(2,1)S(1)}, u32[]{:S(2)}, u32[]{:S(2)}) collective-permute-start(bf16[64,256]{1,0:T(8,128)(2,1)S(1)} %convolution_convert_fusion.5), channel_id=1, source_target_pairs={{2,0},{4,2},{6,4},{8,6},{10,8},{12,10},{14,12},{16,14},{18,16},{20... | collective-permute-start | bytes 98312 | tf_op jit(solution)/shard_map/ppermute | solution.py:13
  17.2 2.1 %convolution_convert_fusion.4 = bf16[64,256]{1,0:T(8,128)(2,1)S(1)} fusion(bf16[1,2,1024,256]{3,2,1,0:T(8,128)(2,1)} %param.4, f32[1024]{0:T(1024)S(1)} %iota_add_fusion, f32[64]{0:T(128)S(1)} %add_multiply_fusion), kind=kOutput, calls=%fused_computation.37 | convolution fusion | flops 33832960 | bytes 561408 | tf_op jit(solution)/shard_map/dot_general | solution.py:23
  19.3 1.3 %collective-permute-start.8 = (bf16[64,256]{1,0:T(8,128)(2,1)S(1)}, bf16[64,256]{1,0:T(8,128)(2,1)S(1)}, u32[]{:S(2)}, u32[]{:S(2)}) collective-permute-start(bf16[64,256]{1,0:T(8,128)(2,1)S(1)} %convolution_convert_fusion.4), channel_id=1, source_target_pairs={{2,0},{4,2},{6,4},{8,6},{10,8},{12,10},{14,12},{16,14},{18,16},{20... | collective-permute-start | bytes 98312 | tf_op jit(solution)/shard_map/ppermute | solution.py:13
  22.4 2.7 %collective-permute-done.8 = bf16[64,256]{1,0:T(8,128)(2,1)S(1)} collective-permute-done((bf16[64,256]{1,0:T(8,128)(2,1)S(1)}, bf16[64,256]{1,0:T(8,128)(2,1)S(1)}, u32[]{:S(2)}, u32[]{:S(2)}) %collective-permute-start.8) | collective-permute-done | bytes 32800 | tf_op jit(solution)/shard_map/ppermute | solution.py:13
  26.4 3.9 %collective-permute-done.9 = bf16[64,256]{1,0:T(8,128)(2,1)S(1)} collective-permute-done((bf16[64,256]{1,0:T(8,128)(2,1)S(1)}, bf16[64,256]{1,0:T(8,128)(2,1)S(1)}, u32[]{:S(2)}, u32[]{:S(2)}) %collective-permute-start.9) | collective-permute-done | bytes 32800 | tf_op jit(solution)/shard_map/ppermute | solution.py:13
  31.7 1.3 collective-permute-start.5
  33.0 2.6 %collective-permute-done.10 = bf16[64,256]{1,0:T(8,128)(2,1)S(1)} collective-permute-done((bf16[64,256]{1,0:T(8,128)(2,1)S(1)}, bf16[64,256]{1,0:T(8,128)(2,1)S(1)}, u32[]{:S(2)}, u32[]{:S(2)}) %collective-permute-start.10) | collective-permute-done | bytes 32800 | tf_op jit(solution)/shard_map/ppermute | solution.py:13
  35.6 1.9 %collective-permute-done.5 = bf16[64,256]{1,0:T(8,128)(2,1)S(1)} collective-permute-done((bf16[64,256]{1,0:T(8,128)(2,1)S(1)}, bf16[64,256]{1,0:T(8,128)(2,1)S(1)}, u32[]{:S(2)}, u32[]{:S(2)}) %collective-permute-start.5) | collective-permute-done | bytes 32800 | tf_op jit(solution)/shard_map/ppermute | solution.py:13
  37.6 2.1 %fusion.16 = bf16[128,1024]{1,0:T(8,128)(2,1)S(1)} fusion(bf16[2,2,1024,1024]{3,2,1,0:T(8,128)(2,1)} %bitcast.79, bf16[64,1024]{1,0:T(8,128)(2,1)S(1)} %get-tuple-element.36, bf16[64,1024]{1,0:T(8,128)(2,1)S(1)} %collective-permute-done), kind=kOutput, calls=%fused_computation.24 | convolution fusion | flops 269090816 | bytes 2621440 | tf_op jit(solution)/shard_map/dot_general | solution.py:23
  40.7 2.1 %fusion.17 = bf16[128,1024]{1,0:T(8,128)(2,1)S(1)} fusion(bf16[2,2,1024,1024]{3,2,1,0:T(8,128)(2,1)} %bitcast.80, bf16[64,1024]{1,0:T(8,128)(2,1)S(1)} %get-tuple-element.36, bf16[64,1024]{1,0:T(8,128)(2,1)S(1)} %collective-permute-done), kind=kOutput, calls=%fused_computation.25 | convolution fusion | flops 269090816 | bytes 2621440 | tf_op jit(solution)/shard_map/dot_general | solution.py:23
  47.2 4.5 %collective-permute-start.14 = (bf16[64,256]{1,0:T(8,128)(2,1)S(1)}, bf16[64,256]{1,0:T(8,128)(2,1)S(1)}, u32[]{:S(2)}, u32[]{:S(2)}) collective-permute-start(bf16[64,256]{1,0:T(8,128)(2,1)S(1)} %get-tuple-element.37), channel_id=1, source_target_pairs={{0,2},{2,4},{4,6},{6,8},{8,10},{10,12},{12,14},{14,16},{16,18},{18... | collective-permute-start | bytes 98312 | tf_op jit(solution)/shard_map/ppermute | solution.py:13
  52.0 3.5 %collective-permute-start.12 = (bf16[64,256]{1,0:T(8,128)(2,1)S(1)}, bf16[64,256]{1,0:T(8,128)(2,1)S(1)}, u32[]{:S(2)}, u32[]{:S(2)}) collective-permute-start(bf16[64,256]{1,0:T(8,128)(2,1)S(1)} %get-tuple-element.41), channel_id=1, source_target_pairs={{0,2},{2,4},{4,6},{6,8},{8,10},{10,12},{12,14},{14,16},{16,18},{18... | collective-permute-start | bytes 98312 | tf_op jit(solution)/shard_map/ppermute | solution.py:13
  56.9 1.5 %collective-permute-start.6 = (bf16[256,1024]{1,0:T(8,128)(2,1)S(1)}, bf16[256,1024]{1,0:T(8,128)(2,1)S(1)}, u32[]{:S(2)}, u32[]{:S(2)}) collective-permute-start(bf16[256,1024]{1,0:T(8,128)(2,1)S(1)} %pad_maximum_fusion.1), channel_id=1, source_target_pairs={{2,0},{4,2},{6,4},{8,6},{10,8},{12,10},{14,12},{16,14},{18,16},{20... | collective-permute-start | bytes 1572872 | tf_op jit(solution)/shard_map/ppermute | solution.py:13
  58.4 4.0 %collective-permute-done.1 = bf16[256,1024]{1,0:T(8,128)(2,1)S(1)} collective-permute-done((bf16[256,1024]{1,0:T(8,128)(2,1)S(1)}, bf16[256,1024]{1,0:T(8,128)(2,1)S(1)}, u32[]{:S(2)}, u32[]{:S(2)}) %collective-permute-start.1) | collective-permute-done | bytes 524320 | tf_op jit(solution)/shard_map/ppermute | solution.py:13
  71.4 10.9 %collective-permute-start.13 = (bf16[64,256]{1,0:T(8,128)(2,1)S(1)}, bf16[64,256]{1,0:T(8,128)(2,1)S(1)}, u32[]{:S(2)}, u32[]{:S(2)}) collective-permute-start(bf16[64,256]{1,0:T(8,128)(2,1)S(1)} %fusion.20), channel_id=1, source_target_pairs={{0,2},{2,4},{4,6},{6,8},{8,10},{10,12},{12,14},{14,16},{16,18},{18... | collective-permute-start | bytes 98312 | tf_op jit(solution)/shard_map/ppermute | solution.py:13
  83.7 1.9 %collective-permute-start.15 = (bf16[64,256]{1,0:T(8,128)(2,1)S(1)}, bf16[64,256]{1,0:T(8,128)(2,1)S(1)}, u32[]{:S(2)}, u32[]{:S(2)}) collective-permute-start(bf16[64,256]{1,0:T(8,128)(2,1)S(1)} %fusion.22), channel_id=1, source_target_pairs={{0,2},{2,4},{4,6},{6,8},{8,10},{10,12},{12,14},{14,16},{16,18},{18... | collective-permute-start | bytes 98312 | tf_op jit(solution)/shard_map/ppermute | solution.py:13
  85.8 1.3 collective-permute-start.7
  96.2 15.4 %reduce-scatter.2.cloned.1.call-done = bf16[512,64]{0,1:T(8,128)(2,1)} async-done(((bf16[1024,64]{0,1:T(8,128)(2,1)}), bf16[512,64]{0,1:T(8,128)(2,1)}) %reduce-scatter.2.cloned.1.call-update) | async-done | bytes 65552 | tf_op jit(solution)/shard_map/reduce_scatter | solution.py:110
  112.4 5.2 %all_gather.3 = bf16[1024,64]{0,1:T(8,128)(2,1)S(1)} all-gather(bf16[512,64]{0,1:T(8,128)(2,1)S(1)} %fusion.37), channel_id=1, replica_groups=mesh['depth'=16,'freq'=2] {'freq'}, dimensions={0}, use_global_device_ids=true | all-gather | bytes 196608 | tf_op jit(solution)/shard_map/all_gather | solution.py:114
  121.1 1.5 %convert_bitcast_fusion = f32[1,512,64]{1,2,0:T(8,128)} fusion(bf16[512,64]{0,1:T(8,128)(2,1)} %reduce-scatter.2.cloned.1.call-done), kind=kLoop, calls=%fused_computation.88 | loop fusion | flops 32768 | bytes 196608 | tf_op jit(solution)/shard_map/broadcast_in_dim | solution.py:117
  (115 shorter events, 35.1 us)
Async XLA Ops:
  7.2 104.4 %reduce-scatter.2.cloned.1.call-start = ((), (), s32[]{:S(2)}) async-start(), calls=%async_computation.1 | async-start | bytes 196608 | tf_op jit(solution)/shard_map/reduce_scatter | solution.py:110
  7.2 36.7 %copy-start.1 = (bf16[1,2,2,1024,1024]{4,3,2,1,0:T(8,128)(2,1)S(1)}, bf16[1,2,2,1024,1024]{4,3,2,1,0:T(8,128)(2,1)}, u32[]{:S(2)}) copy-start(bf16[1,2,2,1024,1024]{4,3,2,1,0:T(8,128)(2,1)} %param.3) | copy-start | bytes 25165828
  9.3 28.3 %collective-permute-start = (bf16[64,1024]{1,0:T(8,128)(2,1)S(1)}, bf16[64,1024]{1,0:T(8,128)(2,1)S(1)}, u32[]{:S(2)}, u32[]{:S(2)}) collective-permute-start(bf16[64,1024]{1,0:T(8,128)(2,1)S(1)} %get-tuple-element.35), channel_id=1, source_target_pairs={{2,0},{4,2},{6,4},{8,6},{10,8},{12,10},{14,12},{16,14},{18,16},{20... | collective-permute-start | bytes 393224 | tf_op jit(solution)/shard_map/ppermute | solution.py:13
  10.7 60.1 %collective-permute-start.11 = (bf16[64,1024]{1,0:T(8,128)(2,1)S(1)}, bf16[64,1024]{1,0:T(8,128)(2,1)S(1)}, u32[]{:S(2)}, u32[]{:S(2)}) collective-permute-start(bf16[64,1024]{1,0:T(8,128)(2,1)S(1)} %get-tuple-element.35), channel_id=1, source_target_pairs={{0,2},{2,4},{4,6},{6,8},{8,10},{10,12},{12,14},{14,16},{16,18},{18... | collective-permute-start | bytes 393224 | tf_op jit(solution)/shard_map/ppermute | solution.py:13
  15.9 5.2 %collective-permute-start.3 = (bf16[64,256]{1,0:T(8,128)(2,1)S(1)}, bf16[64,256]{1,0:T(8,128)(2,1)S(1)}, u32[]{:S(2)}, u32[]{:S(2)}) collective-permute-start(bf16[64,256]{1,0:T(8,128)(2,1)S(1)} %convolution_convert_fusion.5), channel_id=1, source_target_pairs={{2,0},{4,2},{6,4},{8,6},{10,8},{12,10},{14,12},{16,14},{18,16},{20... | collective-permute-start | bytes 98312 | tf_op jit(solution)/shard_map/ppermute | solution.py:13
  19.3 5.8 %collective-permute-start.8 = (bf16[64,256]{1,0:T(8,128)(2,1)S(1)}, bf16[64,256]{1,0:T(8,128)(2,1)S(1)}, u32[]{:S(2)}, u32[]{:S(2)}) collective-permute-start(bf16[64,256]{1,0:T(8,128)(2,1)S(1)} %convolution_convert_fusion.4), channel_id=1, source_target_pairs={{2,0},{4,2},{6,4},{8,6},{10,8},{12,10},{14,12},{16,14},{18,16},{20... | collective-permute-start | bytes 98312 | tf_op jit(solution)/shard_map/ppermute | solution.py:13
  21.1 10.6 %collective-permute-start.4 = (bf16[64,256]{1,0:T(8,128)(2,1)S(1)}, bf16[64,256]{1,0:T(8,128)(2,1)S(1)}, u32[]{:S(2)}, u32[]{:S(2)}) collective-permute-start(bf16[64,256]{1,0:T(8,128)(2,1)S(1)} %collective-permute-done.3), channel_id=1, source_target_pairs={{2,0},{4,2},{6,4},{8,6},{10,8},{12,10},{14,12},{16,14},{18,16},{20... | collective-permute-start | bytes 98312 | tf_op jit(solution)/shard_map/ppermute | solution.py:13
  25.1 5.2 %collective-permute-start.9 = (bf16[64,256]{1,0:T(8,128)(2,1)S(1)}, bf16[64,256]{1,0:T(8,128)(2,1)S(1)}, u32[]{:S(2)}, u32[]{:S(2)}) collective-permute-start(bf16[64,256]{1,0:T(8,128)(2,1)S(1)} %collective-permute-done.8), channel_id=1, source_target_pairs={{2,0},{4,2},{6,4},{8,6},{10,8},{12,10},{14,12},{16,14},{18,16},{20... | collective-permute-start | bytes 98312 | tf_op jit(solution)/shard_map/ppermute | solution.py:13
  30.3 5.2 %collective-permute-start.10 = (bf16[64,256]{1,0:T(8,128)(2,1)S(1)}, bf16[64,256]{1,0:T(8,128)(2,1)S(1)}, u32[]{:S(2)}, u32[]{:S(2)}) collective-permute-start(bf16[64,256]{1,0:T(8,128)(2,1)S(1)} %collective-permute-done.9), channel_id=1, source_target_pairs={{2,0},{4,2},{6,4},{8,6},{10,8},{12,10},{14,12},{16,14},{18,16},{20... | collective-permute-start | bytes 98312 | tf_op jit(solution)/shard_map/ppermute | solution.py:13
  31.7 5.9 %collective-permute-start.5 = (bf16[64,256]{1,0:T(8,128)(2,1)S(1)}, bf16[64,256]{1,0:T(8,128)(2,1)S(1)}, u32[]{:S(2)}, u32[]{:S(2)}) collective-permute-start(bf16[64,256]{1,0:T(8,128)(2,1)S(1)} %collective-permute-done.4), channel_id=1, source_target_pairs={{2,0},{4,2},{6,4},{8,6},{10,8},{12,10},{14,12},{16,14},{18,16},{20... | collective-permute-start | bytes 98312 | tf_op jit(solution)/shard_map/ppermute | solution.py:13
  47.2 11.2 %collective-permute-start.14 = (bf16[64,256]{1,0:T(8,128)(2,1)S(1)}, bf16[64,256]{1,0:T(8,128)(2,1)S(1)}, u32[]{:S(2)}, u32[]{:S(2)}) collective-permute-start(bf16[64,256]{1,0:T(8,128)(2,1)S(1)} %get-tuple-element.37), channel_id=1, source_target_pairs={{0,2},{2,4},{4,6},{6,8},{8,10},{10,12},{12,14},{14,16},{16,18},{18... | collective-permute-start | bytes 98312 | tf_op jit(solution)/shard_map/ppermute | solution.py:13
  52.0 6.4 %collective-permute-start.12 = (bf16[64,256]{1,0:T(8,128)(2,1)S(1)}, bf16[64,256]{1,0:T(8,128)(2,1)S(1)}, u32[]{:S(2)}, u32[]{:S(2)}) collective-permute-start(bf16[64,256]{1,0:T(8,128)(2,1)S(1)} %get-tuple-element.41), channel_id=1, source_target_pairs={{0,2},{2,4},{4,6},{6,8},{8,10},{10,12},{12,14},{14,16},{16,18},{18... | collective-permute-start | bytes 98312 | tf_op jit(solution)/shard_map/ppermute | solution.py:13
  55.5 6.8 %collective-permute-start.1 = (bf16[256,1024]{1,0:T(8,128)(2,1)S(1)}, bf16[256,1024]{1,0:T(8,128)(2,1)S(1)}, u32[]{:S(2)}, u32[]{:S(2)}) collective-permute-start(bf16[256,1024]{1,0:T(8,128)(2,1)S(1)} %pad_maximum_fusion), channel_id=1, source_target_pairs={{2,0},{4,2},{6,4},{8,6},{10,8},{12,10},{14,12},{16,14},{18,16},{20... | collective-permute-start | bytes 1572872 | tf_op jit(solution)/shard_map/ppermute | solution.py:13
  56.9 9.3 %collective-permute-start.6 = (bf16[256,1024]{1,0:T(8,128)(2,1)S(1)}, bf16[256,1024]{1,0:T(8,128)(2,1)S(1)}, u32[]{:S(2)}, u32[]{:S(2)}) collective-permute-start(bf16[256,1024]{1,0:T(8,128)(2,1)S(1)} %pad_maximum_fusion.1), channel_id=1, source_target_pairs={{2,0},{4,2},{6,4},{8,6},{10,8},{12,10},{14,12},{16,14},{18,16},{20... | collective-permute-start | bytes 1572872 | tf_op jit(solution)/shard_map/ppermute | solution.py:13
  71.4 22.7 %collective-permute-start.13 = (bf16[64,256]{1,0:T(8,128)(2,1)S(1)}, bf16[64,256]{1,0:T(8,128)(2,1)S(1)}, u32[]{:S(2)}, u32[]{:S(2)}) collective-permute-start(bf16[64,256]{1,0:T(8,128)(2,1)S(1)} %fusion.20), channel_id=1, source_target_pairs={{0,2},{2,4},{4,6},{6,8},{8,10},{10,12},{12,14},{14,16},{16,18},{18... | collective-permute-start | bytes 98312 | tf_op jit(solution)/shard_map/ppermute | solution.py:13
  83.7 10.2 %collective-permute-start.15 = (bf16[64,256]{1,0:T(8,128)(2,1)S(1)}, bf16[64,256]{1,0:T(8,128)(2,1)S(1)}, u32[]{:S(2)}, u32[]{:S(2)}) collective-permute-start(bf16[64,256]{1,0:T(8,128)(2,1)S(1)} %fusion.22), channel_id=1, source_target_pairs={{0,2},{2,4},{4,6},{6,8},{8,10},{10,12},{12,14},{14,16},{16,18},{18... | collective-permute-start | bytes 98312 | tf_op jit(solution)/shard_map/ppermute | solution.py:13
  85.8 3.8 %collective-permute-start.7 = (bf16[128,1024]{1,0:T(8,128)(2,1)S(1)}, bf16[128,1024]{1,0:T(8,128)(2,1)S(1)}, u32[]{:S(2)}, u32[]{:S(2)}) collective-permute-start(bf16[128,1024]{1,0:T(8,128)(2,1)S(1)} %pad_maximum_fusion.4), channel_id=1, source_target_pairs={{2,0},{4,2},{6,4},{8,6},{10,8},{12,10},{14,12},{16,14},{18,16},{20... | collective-permute-start | bytes 786440 | tf_op jit(solution)/shard_map/ppermute | solution.py:13
  87.4 4.5 %collective-permute-start.2 = (bf16[128,1024]{1,0:T(8,128)(2,1)S(1)}, bf16[128,1024]{1,0:T(8,128)(2,1)S(1)}, u32[]{:S(2)}, u32[]{:S(2)}) collective-permute-start(bf16[128,1024]{1,0:T(8,128)(2,1)S(1)} %pad_maximum_fusion.3), channel_id=1, source_target_pairs={{2,0},{4,2},{6,4},{8,6},{10,8},{12,10},{14,12},{16,14},{18,16},{20... | collective-permute-start | bytes 786440 | tf_op jit(solution)/shard_map/ppermute | solution.py:13
  90.7 20.9 %copy-start = (f32[1,1024,64]{1,2,0:T(8,128)S(1)}, f32[1,1024,64]{1,2,0:T(8,128)}, u32[]{:S(2)}) copy-start(f32[1,1024,64]{1,2,0:T(8,128)} %param.5) | copy-start | bytes 786436
Sparse Core Ops, SparseCore 0:
  95.3 16.2 reduce-scatter.1

commit v2 on v0

v2 whole, which is shorter than its diff:
```python
import functools

import jax
import jax.numpy as jnp
from jax import lax
from jax.experimental import pallas as pl
from jax.experimental.pallas import tpu as pltpu
from jax.sharding import PartitionSpec as P

BF = jnp.bfloat16
F32 = jnp.float32
TILE = 256


def dot(a, b):
    return jnp.dot(a, b, preferred_element_type=F32)


def dot_nt(a, b):
    return lax.dot_general(a, b, (((1,), (1,)), ((), ())), preferred_element_type=F32)


def dot_tn(a, b):
    return lax.dot_general(a, b, (((0,), (0,)), ((), ())), preferred_element_type=F32)


def turned(field):
    half = field.shape[-1] // 2
    return jnp.concatenate([-field[:, half:], field[:, :half]], 1)


def angle_table(count, points):
    angle = lax.broadcasted_iota(jnp.int32, (count, points), 0).astype(F32) + 0.5
    place = lax.broadcasted_iota(jnp.int32, (count, points), 1).astype(F32) + 0.5
    return ((2.0 / points) ** 0.5 * jnp.cos(jnp.pi * angle * place / points)).astype(BF)


def body(
    nd, nf, prop, inc, coef, up_out, grad_out, refl_out,
    w, src, cf, table, k0, k_up, k_dn, a, q, s1, s1_in, s2, g, g1_in, g2_in,
    b0, b_in, e1, e_in, fin, up_v, part_s, part_in, grad_t, grad_v, refl_v,
    in_sem, out_sem, send, recv, fsend, frecv,
):
    me = lax.axis_index("depth")
    fme = lax.axis_index("freq")
    nfreq, _, points, _ = w.shape
    count = table.shape[0]
    half = src.shape[2] // 2
    has_above = me > 0
    has_below = me < nd - 1
    above = lax.rem(me + nd - 1, nd)
    below = lax.rem(me + 1, nd)

    coef_in = pltpu.make_async_copy(coef.at[0], cf, in_sem.at[0])
    src_in = pltpu.make_async_copy(inc.at[0], src, in_sem.at[1])
    w_in = [
        [
            pltpu.make_async_copy(prop.at[0, f, p], w.at[f, p], in_sem.at[2 + 2 * f + p])
            for p in range(2)
        ]
        for f in range(nfreq)
    ]
    coef_in.start()
    for f in range(nfreq):
        w_in[f][0].start()
        w_in[f][1].start()
        if f == 0:
            src_in.start()

    barrier = pltpu.get_barrier_semaphore()

    @pl.when(has_above)
    def _():
        pl.semaphore_signal(barrier, 1, device_id={"depth": above})

    @pl.when(has_below)
    def _():
        pl.semaphore_signal(barrier, 1, device_id={"depth": below})

    for d in range(1, nf):
        pl.semaphore_signal(barrier, 1, device_id={"freq": lax.rem(fme + d, nf)})

    def ahead(x, y, i):
        return pltpu.make_async_remote_copy(
            x, y, send.at[i], recv.at[i], device_id={"depth": above}
        )

    def behind(x, y, i):
        return pltpu.make_async_remote_copy(
            x, y, send.at[i], recv.at[i], device_id={"depth": below}
        )

    c_kup = ahead(k0, k_up, 0)
    c_kdn = behind(k0, k_dn, 1)
    c_a = [ahead(a.at[j], a.at[j + 1], 2 + j) for j in range(3)]
    c_b = behind(b0, b_in, 5)
    c_e = behind(e1, e_in, 6)
    c_s1 = [ahead(s1.at[f], s1_in.at[f], 7 + f) for f in range(nfreq)]
    c_g1 = [
        ahead(g.at[f, pl.ds(4 * count, 2 * count)], g1_in.at[f], 7 + nfreq + f)
        for f in range(nfreq)
    ]
    c_g2 = [
        ahead(g.at[f, pl.ds(2 * count, 2 * count)], g2_in.at[f], 7 + 2 * nfreq + f)
        for f in range(nfreq)
    ]
    ups = [c_kup, *c_a, *c_s1, *c_g1, *c_g2]
    downs = [c_kdn, c_b, c_e]

    def start_up(c):
        pl.when(has_above)(c.start)

    def start_down(c):
        pl.when(has_below)(c.start)

    def take(c, there, ref, i=None):
        pl.when(there)(c.wait_recv)

        @pl.when(jnp.logical_not(there))
        def _():
            if i is None:
                ref[...] = jnp.zeros(ref.shape, ref.dtype)
            else:
                ref[i] = jnp.zeros(ref.shape[1:], ref.dtype)

    table[...] = angle_table(count, points)
    coef_in.wait()
    cf_t = cf[...].T
    k0[...] = (cf_t * table[...].astype(F32)).astype(BF)

    inside = jnp.logical_and(has_above, has_below)
    pl.when(inside)(lambda: pl.semaphore_wait(barrier, nf + 1))
    pl.when(jnp.logical_not(inside))(lambda: pl.semaphore_wait(barrier, nf))
    start_up(c_kup)
    start_down(c_kdn)

    def tiles(step):
        def one(c, carry):
            step(pl.ds(pl.multiple_of(c * TILE, TILE), TILE))
            return carry

        lax.fori_loop(0, points // TILE, one, 0)

    def real_times(rows, f, out, base):
        def step(cols):
            for p in range(2):
                out[f, pl.ds(base + p * count, count), cols] = dot(
                    rows[...], w[f, p, :, cols]
                ).astype(BF)

        tiles(step)

    def complex_times(rows, f, out, base):
        def step(cols):
            x = rows[f]
            first = dot(x, w[f, 0, :, cols])
            second = dot(x, w[f, 1, :, cols])
            out[f, pl.ds(base, count), cols] = (first[:count] - second[count:]).astype(BF)
            out[f, pl.ds(base + count, count), cols] = (first[count:] + second[:count]).astype(BF)

        tiles(step)

    for f in range(nfreq):
        w_in[f][0].wait()
        w_in[f][1].wait()
        real_times(table, f, s1, 0)
        start_up(c_s1[f])
    src_in.wait()
    for f in range(nfreq):
        a[0, f] = dot(table[...], src[f]).astype(BF)
    start_up(c_a[0])

    take(c_kup, has_below, k_up)
    for f in range(nfreq):
        real_times(k_up, f, g, 4 * count)
        start_up(c_g1[f])

    def mixed(pair, field):
        n = pair.shape[1] // 2
        return dot(pair[:, :n], field) + dot(pair[:, n:], turned(field))

    take(c_a[0], has_below, a, 1)
    start_up(c_a[1])
    tg1 = []
    for f in range(nfreq):
        tg1.append(dot_nt(table[...], g[f, pl.ds(4 * count, 2 * count)]).astype(BF))
        b0[f] = mixed(tg1[f], a[1, f]).astype(BF)
    start_down(c_b)

    th1 = []
    for f in range(nfreq):
        take(c_s1[f], has_below, s1_in, f)
        complex_times(s1_in, f, s2, 0)
        th1.append(
            [dot_nt(s1_in[f, pl.ds(p * count, count)], k0[...]).astype(BF) for p in range(2)]
        )
        low = dot(th1[f][0], b0[f]) + dot(th1[f][1], turned(b0[f]))
        d1 = (a[1, f].astype(F32) - low).astype(BF)
        q[f, pl.ds(4 * count, count)] = d1
        q[f, pl.ds(5 * count, count)] = turned(d1)
    take(c_a[1], has_below, a, 2)
    start_up(c_a[2])
    take(c_kdn, has_above, k_dn)
    take(c_b, has_above, b_in)

    for f in range(nfreq):
        take(c_g1[f], has_below, g1_in, f)
        complex_times(g1_in, f, g, 2 * count)
        start_up(c_g2[f])

    for f in range(nfreq):
        tg2 = dot_nt(table[...], g[f, pl.ds(2 * count, 2 * count)]).astype(BF)
        c0 = (mixed(tg2, a[2, f]) + mixed(tg1[f], a[1, f])).astype(BF)
        th2 = [dot_nt(s2[f, pl.ds(p * count, count)], k_dn[...]).astype(BF) for p in range(2)]
        e1[f] = (
            dot(th2[0], b_in[f])
            + dot(th2[1], turned(b_in[f]))
            + dot(th1[f][0], c0)
            + dot(th1[f][1], turned(c0))
        ).astype(BF)
    start_down(c_e)
    take(c_a[2], has_below, a, 3)
    for f in range(nfreq):
        q[f, pl.ds(0, count)] = a[3, f]
        q[f, pl.ds(count, count)] = turned(a[3, f])
        q[f, pl.ds(2 * count, count)] = a[2, f]
        q[f, pl.ds(3 * count, count)] = turned(a[2, f])
    take(c_e, has_above, e_in)
    for f in range(nfreq):
        fin[f] = (a[0, f].astype(F32) - e_in[f].astype(F32)).astype(BF)

    up_copies = []
    for f in range(nfreq):
        take(c_g2[f], has_below, g2_in, f)
        complex_times(g2_in, f, g, 0)

        def field(cols):
            value = dot_tn(g[f, :, cols], q[f]).astype(BF)
            up_v[f, cols] = value
            corr = dot_nt(fin[f], value)
            if f == 0:
                grad_t[:, cols] = corr
            else:
                grad_t[:, cols] += corr

        tiles(field)
        up_copies.append(pltpu.make_async_copy(up_v.at[f], up_out.at[0, f], out_sem.at[f]))
        up_copies[f].start()

    scale = 1.0 / (half * nfreq * nf) ** 0.5
    grad_t[...] = grad_t[...] * scale
    part_s[...] = grad_t[...].astype(BF)
    c_f = [
        pltpu.make_async_remote_copy(
            part_s, part_in.at[d - 1], fsend.at[d - 1], frecv.at[d - 1],
            device_id={"freq": lax.rem(fme + d, nf)},
        )
        for d in range(1, nf)
    ]
    for c in c_f:
        c.start()
    for d, c in enumerate(c_f):
        c.wait_recv()
        grad_t[...] += part_in[d].astype(F32)

    rows = points // nf
    k0_new = ((cf_t - grad_t[...]) * table[...].astype(F32)).astype(BF)
    mine = pl.ds(pl.multiple_of(fme * rows, rows), rows)
    refl_copies = []
    pl.when(has_above)(c_kup.wait_send)
    pl.when(has_below)(c_kdn.wait_send)
    k0[...] = k0_new
    for f in range(nfreq):

        def shine(cols):
            refl_v[f, cols] = dot_tn(k0[:, cols], fin[f]).astype(BF)

        tiles(shine)
        refl_copies.append(
            pltpu.make_async_copy(refl_v.at[f], refl_out.at[0, f], out_sem.at[nfreq + f])
        )
        refl_copies[f].start()
    grad_v[...] = grad_t[:, mine].T
    grad_copy = pltpu.make_async_copy(grad_v, grad_out.at[0], out_sem.at[2 * nfreq])
    grad_copy.start()

    for c in ups[1:]:
        pl.when(has_above)(c.wait_send)
    for c in downs[1:]:
        pl.when(has_below)(c.wait_send)
    for c in c_f:
        c.wait_send()
    for c in (*up_copies, *refl_copies, grad_copy):
        c.wait()


def solution(mesh):
    nd, nf = mesh.shape["depth"], mesh.shape["freq"]

    def local(propagator, incident, coeffs):
        _, nfreq, points, width = incident.shape
        count = coeffs.shape[2]
        rows = points // nf
        field = (nfreq, points, width)
        angles = (nfreq, count, width)
        messages = 7 + 3 * nfreq
        hbm = pl.BlockSpec(memory_space=pl.ANY)
        v = pltpu.VMEM
        return pl.pallas_call(
            functools.partial(body, nd, nf),
            out_shape=(
                jax.ShapeDtypeStruct((1, *field), BF),
                jax.ShapeDtypeStruct((1, rows, count), F32),
                jax.ShapeDtypeStruct((1, *field), BF),
            ),
            in_specs=[hbm] * 3,
            out_specs=[hbm] * 3,
            scratch_shapes=[
                v((nfreq, 2, points, points), BF),
                v(field, BF),
                v((points, count), F32),
                v((count, points), BF),
                v((count, points), BF),
                v((count, points), BF),
                v((count, points), BF),
                v((4, *angles), BF),
                v((nfreq, 6 * count, width), BF),
                v((nfreq, 2 * count, points), BF),
                v((nfreq, 2 * count, points), BF),
                v((nfreq, 2 * count, points), BF),
                v((nfreq, 6 * count, points), BF),
                v((nfreq, 2 * count, points), BF),
                v((nfreq, 2 * count, points), BF),
                v(angles, BF),
                v(angles, BF),
                v(angles, BF),
                v(angles, BF),
                v(angles, BF),
                v(field, BF),
                v((count, points), BF),
                v((max(nf - 1, 1), count, points), BF),
                v((count, points), F32),
                v((rows, count), F32),
                v(field, BF),
                pltpu.SemaphoreType.DMA((2 + 2 * nfreq,)),
                pltpu.SemaphoreType.DMA((2 * nfreq + 1,)),
                pltpu.SemaphoreType.DMA((messages,)),
                pltpu.SemaphoreType.DMA((messages,)),
                pltpu.SemaphoreType.DMA((max(nf - 1, 1),)),
                pltpu.SemaphoreType.DMA((max(nf - 1, 1),)),
            ],
            compiler_params=pltpu.CompilerParams(
                collective_id=0, has_side_effects=True, vmem_limit_bytes=60 * 1024 * 1024
            ),
            name="bremmer",
        )(propagator, incident, coeffs)

    return jax.shard_map(
        local,
        mesh=mesh,
        in_specs=(
            P("depth", "freq", None, None, None),
            P("depth", "freq", None, None),
            P("depth", None, None),
        ),
        out_specs=(
            P("depth", "freq", None, None),
            P("depth", "freq", None),
            P("depth", "freq", None, None),
        ),
        check_vma=False,
    )
```

time: 159 us -> 50.6 us (0.32)
  the two profiles are of different devices: /device:TPU:0 before, /device:TPU:1 now
where the time goes in v2:
time: 50.6 us; the launch traced here: 50.3 us
  Pallas kernels  41.5 us (82%)
  local copies, waits for them, and re-layouts  8.19 us (16%)
  between operations  0.64 us (1%)
    pallas_call x1, Pallas kernels, local(): pl.pallas_call(functools.partial(body, nd, nf), out_shape=(jax.ShapeDtype...  41.5 us
    unnamed x3, local copies, waits for them, and re-layouts  6.47 us
    pallas_call x1, local copies, waits for them, and re-layouts, local(): pl.pallas_call(functools.partial(body, nd, nf), out_shape=(jax.ShapeDtype...  1.72 us

profile of v2, /device:TPU:1, one launch (start us, length us, event | category | flops | bytes accessed | tf_op | source)
XLA Modules:
  0.0 50.3 jit_solution(6110418318372422363)
XLA Ops:
  0.6 1.9 %copy.6.coef = f32[1,1024,64]{2,1,0:T(8,128)} copy(f32[1,1024,64]{1,2,0:T(8,128)} %param.5) | data formatting | bytes 524288 | tf_op args[2]
  2.6 41.5 %bremmer.1 = (bf16[1,2,1024,256]{3,2,1,0:T(8,128)(2,1)}, f32[1,512,64]{2,1,0:T(8,128)}, bf16[1,2,1024,256]{3,2,1,0:T(8,128)(2,1)}) custom-call(bf16[1,2,2,1024,1024]{4,3,2,1,0:T(8,128)(2,1)} %prop.1, bf16[1,2,1024,256]{3,2,1,0:T(8,128)(2,1)} %inc.1, f32[1,1024,64]{2,1,0:T(8,128)} %copy.6.coef), custom_call_target="tpu_custom_call" | custom-call | tf_op jit(solution)/shard_map/bremmer/pallas_call | solution.py:309
  44.1 1.7 %copy.7 = f32[1,512,64]{1,2,0:T(8,128)} copy(f32[1,512,64]{2,1,0:T(8,128)} %get-tuple-element.4) | data formatting | bytes 262144 | tf_op jit(solution)/shard_map/bremmer/pallas_call | solution.py:309
  45.8 2.3 %copy.10 = bf16[1,2,1024,256]{3,2,1,0:T(8,128)(2,1)} copy(bf16[1,2,1024,256]{3,2,1,0:T(8,128)(2,1)} %get-tuple-element.9) | data formatting | bytes 2097152
  48.1 2.3 %copy.11 = bf16[1,2,1024,256]{3,2,1,0:T(8,128)(2,1)} copy(bf16[1,2,1024,256]{3,2,1,0:T(8,128)(2,1)} %get-tuple-element.11) | data formatting | bytes 2097152

commit v3 on v2

--- a/solution.py
+++ b/solution.py
@@ -36,9 +36,9 @@
 
 
 def body(
-    nd, nf, prop, inc, coef, up_out, grad_out, refl_out,
+    nd, nf, prop, inc, coef, up_out, grad_out, kernel_out, fin_out,
     w, src, cf, table, k0, k_up, k_dn, a, q, s1, s1_in, s2, g, g1_in, g2_in,
-    b0, b_in, e1, e_in, fin, up_v, part_s, part_in, grad_t, grad_v, refl_v,
+    b0, b_in, e1, e_in, fin, up_v, part_s, part_in, grad_t,
     in_sem, out_sem, send, recv, fsend, frecv,
 ):
     me = lax.axis_index("depth")
@@ -61,11 +61,10 @@
         for f in range(nfreq)
     ]
     coef_in.start()
+    src_in.start()
     for f in range(nfreq):
         w_in[f][0].start()
         w_in[f][1].start()
-        if f == 0:
-            src_in.start()
 
     barrier = pltpu.get_barrier_semaphore()
 
@@ -125,8 +124,7 @@
 
     table[...] = angle_table(count, points)
     coef_in.wait()
-    cf_t = cf[...].T
-    k0[...] = (cf_t * table[...].astype(F32)).astype(BF)
+    k0[...] = (cf[...] * table[...].astype(F32)).astype(BF)
 
     inside = jnp.logical_and(has_above, has_below)
     pl.when(inside)(lambda: pl.semaphore_wait(barrier, nf + 1))
@@ -160,27 +158,32 @@
 
         tiles(step)
 
+    src_in.wait()
+    for f in range(nfreq):
+        a[0, f] = dot(table[...], src[f]).astype(BF)
+    start_up(c_a[0])
+
     for f in range(nfreq):
         w_in[f][0].wait()
         w_in[f][1].wait()
         real_times(table, f, s1, 0)
         start_up(c_s1[f])
-    src_in.wait()
-    for f in range(nfreq):
-        a[0, f] = dot(table[...], src[f]).astype(BF)
-    start_up(c_a[0])
-
+        if f == 0:
+            take(c_a[0], has_below, a, 1)
+            start_up(c_a[1])
     take(c_kup, has_below, k_up)
+
     for f in range(nfreq):
         real_times(k_up, f, g, 4 * count)
         start_up(c_g1[f])
+        if f == 0:
+            take(c_a[1], has_below, a, 2)
+            start_up(c_a[2])
 
     def mixed(pair, field):
         n = pair.shape[1] // 2
         return dot(pair[:, :n], field) + dot(pair[:, n:], turned(field))
 
-    take(c_a[0], has_below, a, 1)
-    start_up(c_a[1])
     tg1 = []
     for f in range(nfreq):
         tg1.append(dot_nt(table[...], g[f, pl.ds(4 * count, 2 * count)]).astype(BF))
@@ -198,16 +201,14 @@
         d1 = (a[1, f].astype(F32) - low).astype(BF)
         q[f, pl.ds(4 * count, count)] = d1
         q[f, pl.ds(5 * count, count)] = turned(d1)
-    take(c_a[1], has_below, a, 2)
-    start_up(c_a[2])
-    take(c_kdn, has_above, k_dn)
-    take(c_b, has_above, b_in)
 
     for f in range(nfreq):
         take(c_g1[f], has_below, g1_in, f)
         complex_times(g1_in, f, g, 2 * count)
         start_up(c_g2[f])
 
+    take(c_kdn, has_above, k_dn)
+    take(c_b, has_above, b_in)
     for f in range(nfreq):
         tg2 = dot_nt(table[...], g[f, pl.ds(2 * count, 2 * count)]).astype(BF)
         c0 = (mixed(tg2, a[2, f]) + mixed(tg1[f], a[1, f])).astype(BF)
@@ -228,6 +229,8 @@
     take(c_e, has_above, e_in)
     for f in range(nfreq):
         fin[f] = (a[0, f].astype(F32) - e_in[f].astype(F32)).astype(BF)
+    fin_copy = pltpu.make_async_copy(fin, fin_out, out_sem.at[nfreq + 2])
+    fin_copy.start()
 
     up_copies = []
     for f in range(nfreq):
@@ -264,33 +267,50 @@
         grad_t[...] += part_in[d].astype(F32)
 
     rows = points // nf
-    k0_new = ((cf_t - grad_t[...]) * table[...].astype(F32)).astype(BF)
     mine = pl.ds(pl.multiple_of(fme * rows, rows), rows)
-    refl_copies = []
-    pl.when(has_above)(c_kup.wait_send)
-    pl.when(has_below)(c_kdn.wait_send)
-    k0[...] = k0_new
-    for f in range(nfreq):
-
-        def shine(cols):
-            refl_v[f, cols] = dot_tn(k0[:, cols], fin[f]).astype(BF)
-
-        tiles(shine)
-        refl_copies.append(
-            pltpu.make_async_copy(refl_v.at[f], refl_out.at[0, f], out_sem.at[nfreq + f])
-        )
-        refl_copies[f].start()
-    grad_v[...] = grad_t[:, mine].T
-    grad_copy = pltpu.make_async_copy(grad_v, grad_out.at[0], out_sem.at[2 * nfreq])
-    grad_copy.start()
-
-    for c in ups[1:]:
-        pl.when(has_above)(c.wait_send)
-    for c in downs[1:]:
-        pl.when(has_below)(c.wait_send)
     for c in c_f:
         c.wait_send()
-    for c in (*up_copies, *refl_copies, grad_copy):
+    part_s[...] = ((cf[...] - grad_t[...]) * table[...].astype(F32)).astype(BF)
+    last = [
+        pltpu.make_async_copy(part_s, kernel_out, out_sem.at[nfreq]),
+        pltpu.make_async_copy(grad_t.at[:, mine], grad_out.at[0], out_sem.at[nfreq + 1]),
+        fin_copy,
+    ]
+    last[0].start()
+    last[1].start()
+
+    for c in ups:
+        pl.when(has_above)(c.wait_send)
+    for c in downs:
+        pl.when(has_below)(c.wait_send)
+    for c in (*up_copies, *last):
+        c.wait()
+
+
+def shine(up, grad, kernel, fin, up_out, grad_out, refl_out, up_v, grad_v, kt, fv, refl_v, sem, osem):
+    nfreq, points, _ = up_v.shape
+    first = [
+        pltpu.make_async_copy(kernel, kt, sem.at[0]),
+        pltpu.make_async_copy(fin, fv, sem.at[1]),
+        pltpu.make_async_copy(up.at[0], up_v, sem.at[2]),
+        pltpu.make_async_copy(grad, grad_v, sem.at[3]),
+    ]
+    for c in first:
+        c.start()
+    first[0].wait()
+    first[1].wait()
+    last = []
+    for f in range(nfreq):
+        refl_v[f] = dot_tn(kt[...], fv[f]).astype(BF)
+        last.append(pltpu.make_async_copy(refl_v.at[f], refl_out.at[0, f], osem.at[f]))
+        last[f].start()
+    first[2].wait()
+    last.append(pltpu.make_async_copy(up_v, up_out.at[0], osem.at[nfreq]))
+    last[-1].start()
+    first[3].wait()
+    last.append(pltpu.make_async_copy(grad_v, grad_out, osem.at[nfreq + 1]))
+    last[-1].start()
+    for c in last:
         c.wait()
 
 
@@ -306,19 +326,20 @@
         messages = 7 + 3 * nfreq
         hbm = pl.BlockSpec(memory_space=pl.ANY)
         v = pltpu.VMEM
-        return pl.pallas_call(
+        up, grad, kernel, fin = pl.pallas_call(
             functools.partial(body, nd, nf),
             out_shape=(
                 jax.ShapeDtypeStruct((1, *field), BF),
-                jax.ShapeDtypeStruct((1, rows, count), F32),
-                jax.ShapeDtypeStruct((1, *field), BF),
+                jax.ShapeDtypeStruct((1, count, rows), F32),
+                jax.ShapeDtypeStruct((count, points), BF),
+                jax.ShapeDtypeStruct(angles, BF),
             ),
             in_specs=[hbm] * 3,
-            out_specs=[hbm] * 3,
+            out_specs=[hbm] * 4,
             scratch_shapes=[
                 v((nfreq, 2, points, points), BF),
                 v(field, BF),
-                v((points, count), F32),
+                v((count, points), F32),
                 v((count, points), BF),
                 v((count, points), BF),
                 v((count, points), BF),
@@ -340,10 +361,8 @@
                 v((count, points), BF),
                 v((max(nf - 1, 1), count, points), BF),
                 v((count, points), F32),
-                v((rows, count), F32),
-                v(field, BF),
                 pltpu.SemaphoreType.DMA((2 + 2 * nfreq,)),
-                pltpu.SemaphoreType.DMA((2 * nfreq + 1,)),
+                pltpu.SemaphoreType.DMA((nfreq + 3,)),
                 pltpu.SemaphoreType.DMA((messages,)),
                 pltpu.SemaphoreType.DMA((messages,)),
                 pltpu.SemaphoreType.DMA((max(nf - 1, 1),)),
@@ -353,7 +372,29 @@
                 collective_id=0, has_side_effects=True, vmem_limit_bytes=60 * 1024 * 1024
             ),
             name="bremmer",
-        )(propagator, incident, coeffs)
+        )(propagator, incident, jnp.swapaxes(coeffs, 1, 2))
+        up, grad, reflected = pl.pallas_call(
+            shine,
+            out_shape=(
+                jax.ShapeDtypeStruct((1, *field), BF),
+                jax.ShapeDtypeStruct((1, count, rows), F32),
+                jax.ShapeDtypeStruct((1, *field), BF),
+            ),
+            in_specs=[hbm] * 4,
+            out_specs=[hbm] * 3,
+            scratch_shapes=[
+                v(field, BF),
+                v((1, count, rows), F32),
+                v((count, points), BF),
+                v(angles, BF),
+                v(field, BF),
+                pltpu.SemaphoreType.DMA((4,)),
+                pltpu.SemaphoreType.DMA((nfreq + 2,)),
+            ],
+            compiler_params=pltpu.CompilerParams(vmem_limit_bytes=60 * 1024 * 1024),
+            name="shine",
+        )(up, grad, kernel, fin)
+        return up, jnp.swapaxes(grad, 1, 2), reflected
 
     return jax.shard_map(
         local,

time: 50.6 us -> 43.7 us (0.86)
  the two profiles are of different devices: /device:TPU:1 before, /device:TPU:19 now
where the time goes in v3:
time: 43.7 us; the launch traced here: 43.6 us
  Pallas kernels  43 us (98%)
  between operations  0.64 us (1%)
    pallas_call x1, Pallas kernels, local(): pl.pallas_call(functools.partial(body, nd, nf), out_shape=(jax.ShapeDtype...  40.2 us
    pallas_call x1, Pallas kernels, local(): pl.pallas_call(shine, out_shape=(jax.ShapeDtypeStruct((1, *field), BF), j...  2.79 us

profile of v3, /device:TPU:19, one launch (start us, length us, event | category | flops | bytes accessed | tf_op | source)
XLA Modules:
  0.0 43.6 jit_solution(14239973359370213385)
XLA Ops:
  0.6 40.2 %bremmer.1 = (bf16[1,2,1024,256]{3,2,1,0:T(8,128)(2,1)}, f32[1,64,512]{2,1,0:T(8,128)}, bf16[64,1024]{1,0:T(8,128)(2,1)}, bf16[2,64,256]{2,1,0:T(8,128)(2,1)}) custom-call(bf16[1,2,2,1024,1024]{4,3,2,1,0:T(8,128)(2,1)} %prop.1, bf16[1,2,1024,256]{3,2,1,0:T(8,128)(2,1)} %inc.1, f32[1,64,1024]{2,1,0:T(8,128)} %bitcast.2), custom_call_target="tpu_custom_call" | custom-call | tf_op jit(solution)/shard_map/bremmer/pallas_call | solution.py:329
  40.8 2.8 %shine.1 = (bf16[1,2,1024,256]{3,2,1,0:T(8,128)(2,1)}, f32[1,64,512]{2,1,0:T(8,128)}, bf16[1,2,1024,256]{3,2,1,0:T(8,128)(2,1)}) custom-call(bf16[1,2,1024,256]{3,2,1,0:T(8,128)(2,1)} %get-tuple-element.10.up, f32[1,64,512]{2,1,0:T(8,128)} %get-tuple-element.11.grad, bf16[64,1024]{1,0:T(8,128)(2,1)} %get-tuple-element.12.kernel, ...), custom_call_target="tpu_custom_call" | custom-call | tf_op jit(solution)/shard_map/shine/pallas_call | solution.py:376

commit v4 on v3

--- a/solution.py
+++ b/solution.py
@@ -9,7 +9,7 @@
 
 BF = jnp.bfloat16
 F32 = jnp.float32
-TILE = 256
+TILE = 512
 
 
 def dot(a, b):
@@ -137,7 +137,7 @@
             step(pl.ds(pl.multiple_of(c * TILE, TILE), TILE))
             return carry
 
-        lax.fori_loop(0, points // TILE, one, 0)
+        lax.fori_loop(0, points // TILE, one, 0, unroll=True)
 
     def real_times(rows, f, out, base):
         def step(cols):
@@ -145,6 +145,19 @@
                 out[f, pl.ds(base + p * count, count), cols] = dot(
                     rows[...], w[f, p, :, cols]
                 ).astype(BF)
+
+        tiles(step)
+
+    def second_times(f):
+        def step(cols):
+            x = jnp.concatenate([s1_in[f], g1_in[f]], 0)
+            y = dot(x, w[f, 0, :, cols])
+            z = dot(x, w[f, 1, :, cols])
+            n = count
+            s2[f, pl.ds(0, n), cols] = (y[:n] - z[n : 2 * n]).astype(BF)
+            s2[f, pl.ds(n, n), cols] = (y[n : 2 * n] + z[:n]).astype(BF)
+            g[f, pl.ds(2 * n, n), cols] = (y[2 * n : 3 * n] - z[3 * n :]).astype(BF)
+            g[f, pl.ds(3 * n, n), cols] = (y[3 * n :] + z[2 * n : 3 * n]).astype(BF)
 
         tiles(step)
 
@@ -193,7 +206,9 @@
     th1 = []
     for f in range(nfreq):
         take(c_s1[f], has_below, s1_in, f)
-        complex_times(s1_in, f, s2, 0)
+        take(c_g1[f], has_below, g1_in, f)
+        second_times(f)
+        start_up(c_g2[f])
         th1.append(
             [dot_nt(s1_in[f, pl.ds(p * count, count)], k0[...]).astype(BF) for p in range(2)]
         )
@@ -201,11 +216,6 @@
         d1 = (a[1, f].astype(F32) - low).astype(BF)
         q[f, pl.ds(4 * count, count)] = d1
         q[f, pl.ds(5 * count, count)] = turned(d1)
-
-    for f in range(nfreq):
-        take(c_g1[f], has_below, g1_in, f)
-        complex_times(g1_in, f, g, 2 * count)
-        start_up(c_g2[f])
 
     take(c_kdn, has_above, k_dn)
     take(c_b, has_above, b_in)

time: 43.7 us -> 40.2 us (0.920)
  Pallas kernels: 43 us -> 39.4 us
    pallas_call x1, Pallas kernels: 40.2 us -> 36.6 us  [local(): pl.pallas_call(functools.partial(body, nd, nf), out_shape=(jax.ShapeDtype...]
where the time goes in v4:
time: 40.2 us; the launch traced here: 40.1 us
  Pallas kernels  39.4 us (98%)
  between operations  0.64 us (2%)
    pallas_call x1, Pallas kernels, local(): pl.pallas_call(functools.partial(body, nd, nf), out_shape=(jax.ShapeDtype...  36.6 us
    pallas_call x1, Pallas kernels, local(): pl.pallas_call(shine, out_shape=(jax.ShapeDtypeStruct((1, *field), BF), j...  2.79 us

profile of v4, /device:TPU:19, one launch (start us, length us, event | category | flops | bytes accessed | tf_op | source)
XLA Modules:
  0.0 40.1 jit_solution(4132257424504534451)
XLA Ops:
  0.6 36.6 %bremmer.1 = (bf16[1,2,1024,256]{3,2,1,0:T(8,128)(2,1)}, f32[1,64,512]{2,1,0:T(8,128)}, bf16[64,1024]{1,0:T(8,128)(2,1)}, bf16[2,64,256]{2,1,0:T(8,128)(2,1)}) custom-call(bf16[1,2,2,1024,1024]{4,3,2,1,0:T(8,128)(2,1)} %prop.1, bf16[1,2,1024,256]{3,2,1,0:T(8,128)(2,1)} %inc.1, f32[1,64,1024]{2,1,0:T(8,128)} %bitcast.2), custom_call_target="tpu_custom_call" | custom-call | tf_op jit(solution)/shard_map/bremmer/pallas_call | solution.py:339
  37.3 2.8 %shine.1 = (bf16[1,2,1024,256]{3,2,1,0:T(8,128)(2,1)}, f32[1,64,512]{2,1,0:T(8,128)}, bf16[1,2,1024,256]{3,2,1,0:T(8,128)(2,1)}) custom-call(bf16[1,2,1024,256]{3,2,1,0:T(8,128)(2,1)} %get-tuple-element.10.up, f32[1,64,512]{2,1,0:T(8,128)} %get-tuple-element.11.grad, bf16[64,1024]{1,0:T(8,128)(2,1)} %get-tuple-element.12.kernel, ...), custom_call_target="tpu_custom_call" | custom-call | tf_op jit(solution)/shard_map/shine/pallas_call | solution.py:386
